TPU v7x, 256 devices: a whole 4x4x8 slice. The times are simulated.
256 devices in a mesh: op: 16 (over x_lo, y, core), sec: 16 (over x_hi, z).
Axes of the slice: x: 4 (x_hi: 2, x_lo: 2; x = x_hi * 2 + x_lo), y: 4, z: 8, core: 2. Of those that a mesh axis runs over, the one named last changes fastest.
Arguments:
- psi: bfloat16 [16, 512, 512], P('sec'), may hold values from -6 to 6
- left_env: bfloat16 [128, 16, 512, 512], P('op', 'sec'), may hold values from -0.375 to 0.375
- right_env: bfloat16 [128, 16, 512, 512], P('op', 'sec'), may hold values from -0.25 to 0.25
- pair_code: int32 [128], P('op'), may hold values from 0 to 2
- sketch: bfloat16 [16, 512, 128], P('sec'), may hold values from -0.25 to 0.25
Outputs:
- sigma: bfloat16 [512, 8192], P('op', 'sec')
- basis: float32 [512, 2048], P('op', 'sec')
All inputs are finite; a program needn't handle non-finite values.
Results may differ from a plain program's by a relative error of at most 0.0055.
Values may be sent and summed in bfloat16 or wider, within the bound.
No kernel may reach another device: no remote copies, remote signals or barrier semaphores. Data moves between devices by JAX's collectives and lax.ppermute only.
A program may use at most 64 MiB of HBM per device.

v0:
```python
import math

import jax
import jax.numpy as jnp
from jax import lax
from jax.sharding import PartitionSpec as P


def padded_2(block, sides, width):
    for axis, dim in sides:
        count = lax.axis_size(axis)
        forward = [(i, i + 1) for i in range(count - 1)]
        backward = [(target, source) for source, target in forward]
        low = lax.ppermute(
            lax.slice_in_dim(block, block.shape[dim] - width, None, axis=dim), axis, forward
        )
        high = lax.ppermute(lax.slice_in_dim(block, 0, width, axis=dim), axis, backward)
        block = jnp.concatenate([low, block, high], axis=dim)
    return block


def range_basis(sigma_rows, sketch, width):
    count = sigma_rows.shape[0]
    sec_dev = sketch.shape[0]
    sampled = jnp.einsum(
        "ajd,jdk->jak",
        sigma_rows.reshape(count, sec_dev, width),
        sketch,
        preferred_element_type=jnp.float32,
    )
    return sampled


def finish_basis(sampled, gram, width):
    lower = jnp.linalg.cholesky(gram)
    solved = lax.linalg.triangular_solve(
        lower, sampled, left_side=False, lower=True, transpose_a=True
    )
    sec_dev, count, cols = solved.shape
    return math.sqrt(width) * solved.transpose(1, 0, 2).reshape(count, sec_dev * cols)


def body(psi, left_env, right_env, pair_code, sketch):
    t_dev, sec_dev, width, unused = left_env.shape
    n_op = lax.axis_size("op")
    rows = width // n_op
    scale = 1.0 / math.sqrt(t_dev * n_op)
    padded = padded_2(psi, (("sec", 0),), 1)

    def one_term(index, total):
        code = pair_code[index]
        source = lax.dynamic_slice_in_dim(padded, 2 - code, sec_dev, 0)
        left_rows = left_env[index]
        inner = jnp.einsum(
            "jab,jbc->jac", left_rows, source, preferred_element_type=jnp.float32
        ).astype(jnp.bfloat16)
        return total + scale * jnp.einsum(
            "jac,jcd->jad", inner, right_env[index], preferred_element_type=jnp.float32
        )

    total = lax.fori_loop(
        0, t_dev, one_term, jnp.zeros((sec_dev, lax.axis_size("op") * rows, width), jnp.float32)
    )
    summed = lax.psum_scatter(
        total.transpose(1, 0, 2).reshape(lax.axis_size("op") * rows, sec_dev * width),
        "op",
        scatter_dimension=0,
        tiled=True,
    )
    sigma_rows = summed.astype(jnp.bfloat16)
    sampled = range_basis(sigma_rows, sketch, width)
    gram_part = jnp.einsum("jak,jal->jkl", sampled, sampled, precision=lax.Precision.HIGHEST)
    gram = lax.psum(gram_part, "op")
    basis = finish_basis(sampled, gram, width)
    return (sigma_rows, basis)


def solution(mesh):
    in_specs = (
        P("sec", None, None),
        P("op", "sec", None, None),
        P("op", "sec", None, None),
        P("op"),
        P("sec", None, None),
    )
    out_specs = (P("op", "sec"), P("op", "sec"))
    return jax.shard_map(body, mesh=mesh, in_specs=in_specs, out_specs=out_specs, check_vma=False)
```

profile of v0, /device:TPU:5, one launch (start us, length us, event | category | flops | bytes accessed | tf_op | source)
XLA Modules:
  0.0 272.6 jit_solution(13141491743284272402)
XLA Ops:
  7.2 0.0 copy-start
  7.2 0.0 reduce-scatter.2.cloned.1.call-start
  7.2 3.5 %collective-permute-start = (bf16[1,512,512]{2,1,0:T(8,128)(2,1)}, bf16[1,512,512]{2,1,0:T(8,128)(2,1)S(1)}, u32[]{:S(2)}, u32[]{:S(2)}) collective-permute-start(bf16[1,512,512]{2,1,0:T(8,128)(2,1)} %param.7), channel_id=1, source_target_pairs={{0,1},{1,2},{2,3},{3,4},{4,5},{5,6},{6,7},{7,8},{8,9},{9,10},{10,1... | collective-permute-start | bytes 1572872 | tf_op jit(solution)/shard_map/ppermute | solution.py:14
  10.8 5.8 %collective-permute-start.1 = (bf16[1,512,512]{2,1,0:T(8,128)(2,1)}, bf16[1,512,512]{2,1,0:T(8,128)(2,1)}, u32[]{:S(2)}, u32[]{:S(2)}) collective-permute-start(bf16[1,512,512]{2,1,0:T(8,128)(2,1)} %param.7), channel_id=1, source_target_pairs={{1,0},{2,1},{3,2},{4,3},{5,4},{6,5},{7,6},{8,7},{9,8},{10,9},{11,1... | collective-permute-start | bytes 1572872 | tf_op jit(solution)/shard_map/ppermute | solution.py:17
  16.6 0.0 copy-start.3
  16.6 9.9 %collective-permute-done = bf16[1,512,512]{2,1,0:T(8,128)(2,1)S(1)} collective-permute-done((bf16[1,512,512]{2,1,0:T(8,128)(2,1)}, bf16[1,512,512]{2,1,0:T(8,128)(2,1)S(1)}, u32[]{:S(2)}, u32[]{:S(2)}) %collective-permute-start) | collective-permute-done | bytes 524320 | tf_op jit(solution)/shard_map/ppermute | solution.py:14
  26.5 1.0 collective-permute-done.1
  27.5 1.4 pad_maximum_fusion
  28.9 0.0 copy-done.3
  28.9 31.5 %while.16 = (s32[]{:T(128)}, f32[1,512,512]{2,1,0:T(8,128)S(1)}, bf16[8,1,512,512]{3,2,1,0:T(8,128)(2,1)}, s32[8]{0:T(128)S(1)}, bf16[3,512,512]{2,1,0:T(8,128)(...) while((s32[]{:T(128)}, f32[1,512,512]{2,1,0:T(8,128)S(1)}, ...), condition=%wide.region_1.0_spmd.clone, body=%wide.region_0.0_spmd.clone.sunk | while | flops 537919488 | bytes 3671213 | solution.py:61
  28.9 0.6 dynamic_slice.65
  30.8 2.0 fusion.30
  32.8 0.6 dynamic_slice.65
  34.7 2.0 fusion.30
  36.8 0.6 dynamic_slice.65
  38.7 2.0 fusion.30
  40.7 0.6 dynamic_slice.65
  42.6 2.0 fusion.30
  44.6 0.6 dynamic_slice.65
  46.5 2.0 fusion.30
  48.6 0.6 dynamic_slice.65
  50.5 2.0 fusion.30
  52.5 0.6 dynamic_slice.65
  54.4 2.0 fusion.30
  56.4 0.6 dynamic_slice.65
  58.3 2.0 fusion.30
  60.4 0.0 copy-start.1
  60.4 1.0 copy-done.1
  61.4 0.0 reduce-scatter.2.cloned.1.call-update
  61.4 0.0 all-reduce.2.cloned.1.call-start
  61.4 63.6 %reduce-scatter.2.cloned.1.call-done = f32[32,512]{1,0:T(8,128)} async-done(((f32[512,512]{1,0:T(8,128)}), f32[32,512]{1,0:T(8,128)}) %reduce-scatter.2.cloned.1.call-update) | async-done | bytes 65552 | tf_op jit(solution)/shard_map/reduce_scatter | solution.py:64
  125.0 0.8 convert_element_type.14
  125.8 0.0 copy-done
  125.8 0.0 copy-start.2
  125.8 0.1 fusion.14
  126.0 0.9 convolution_bitcast_fusion
  126.9 0.0 all-reduce.2.cloned.1.call-update
  126.9 113.4 %all-reduce.2.cloned.1.call-done = f32[1,128,128]{1,2,0:T(8,128)} async-done(((f32[1,128,128]{1,2,0:T(8,128)}), f32[1,128,128]{1,2,0:T(8,128)}) %all-reduce.2.cloned.1.call-update) | async-done | bytes 65552 | tf_op jit(solution)/shard_map/psum | solution.py:73
  240.4 0.9 copy.8
  241.3 0.9 fusion.18
  242.2 11.7 %custom-call.7 = f32[1,128,128]{2,1,0:T(8,128)S(1)} custom-call(f32[1,128,128]{2,1,0:T(8,128)S(1)} %fusion.18), custom_call_target="Cholesky" | custom-call | tf_op jit(solution)/shard_map/jit(cholesky)/cholesky | solution.py:35
  253.9 0.6 compare_reduce_fusion
  254.5 0.7 fusion.16
  255.2 9.8 %custom-call.8 = f32[1,1,128,128]{2,3,1,0:T(8,128)S(1)} custom-call(f32[1,1,128,128]{3,2,1,0:T(8,128)S(1)} %fusion.16), custom_call_target="InvertDiagBlocksLowerTriangular" | custom-call | tf_op jit(solution)/shard_map/triangular_solve | solution.py:36
  265.0 0.8 convolution_multiply_fusion.1
  265.8 0.0 copy-done.2
  (2 shorter events, 0.0 us)
Async XLA Ops:
  7.2 118.7 %copy-start = (bf16[1,512,128]{2,1,0:T(8,128)(2,1)S(1)}, bf16[1,512,128]{2,1,0:T(8,128)(2,1)}, u32[]{:S(2)}) copy-start(bf16[1,512,128]{2,1,0:T(8,128)(2,1)} %param.11) | copy-start | bytes 393220
  7.2 117.8 %reduce-scatter.2.cloned.1.call-start = ((), (), s32[]{:S(2)}) async-start(), calls=%async_computation.1 | async-start | bytes 1114112 | tf_op jit(solution)/shard_map/reduce_scatter | solution.py:64
  7.2 19.3 %collective-permute-start = (bf16[1,512,512]{2,1,0:T(8,128)(2,1)}, bf16[1,512,512]{2,1,0:T(8,128)(2,1)S(1)}, u32[]{:S(2)}, u32[]{:S(2)}) collective-permute-start(bf16[1,512,512]{2,1,0:T(8,128)(2,1)} %param.7), channel_id=1, source_target_pairs={{0,1},{1,2},{2,3},{3,4},{4,5},{5,6},{6,7},{7,8},{8,9},{9,10},{10,1... | collective-permute-start | bytes 1572872 | tf_op jit(solution)/shard_map/ppermute | solution.py:14
  10.8 16.7 %collective-permute-start.1 = (bf16[1,512,512]{2,1,0:T(8,128)(2,1)}, bf16[1,512,512]{2,1,0:T(8,128)(2,1)}, u32[]{:S(2)}, u32[]{:S(2)}) collective-permute-start(bf16[1,512,512]{2,1,0:T(8,128)(2,1)} %param.7), channel_id=1, source_target_pairs={{1,0},{2,1},{3,2},{4,3},{5,4},{6,5},{7,6},{8,7},{9,8},{10,9},{11,1... | collective-permute-start | bytes 1572872 | tf_op jit(solution)/shard_map/ppermute | solution.py:17
  16.6 12.3 %copy-start.3 = (s32[8]{0:T(128)S(1)}, s32[8]{0:T(128)}, u32[]{:S(2)}) copy-start(s32[8]{0:T(128)} %param.10) | copy-start | bytes 100
  60.4 1.0 copy-start.1
  61.4 179.0 %all-reduce.2.cloned.1.call-start = ((), (), s32[]{:S(2)}) async-start(), calls=%async_computation.2 | async-start | bytes 131072 | tf_op jit(solution)/shard_map/psum | solution.py:73
  125.8 140.0 %copy-start.2 = (bf16[32,512]{1,0:T(8,128)(2,1)}, bf16[32,512]{1,0:T(8,128)(2,1)S(1)}, u32[]{:S(2)}) copy-start(bf16[32,512]{1,0:T(8,128)(2,1)S(1)} %convert_element_type.14) | copy-start | bytes 98308
Sparse Core Ops, SparseCore 0:
  61.5 63.4 reduce-scatter.1
  127.6 112.7 all-reduce.1
where the time goes:
time: 276 us; the launch traced here: 273 us
  waiting for transfers between devices  188 us (68%)
  other arithmetic  25.9 us (9%)
  matrix products  18 us (7%)
  between operations  14.1 us (5%)
  loops' own time  10.6 us (4%)
  starting transfers between devices  9.43 us (3%)
  local copies, waits for them, and re-layouts  6.61 us (2%)
    psum x1, waiting for transfers between devices, body(): gram = lax.psum(gram_part, 'op')  113 us
    reduce_scatter x1, waiting for transfers between devices, body(): lax.psum_scatter(total.transpose(1, 0, 2).reshape(lax.axis_size('op') * r...  63.6 us
    dot_general x8, matrix products, one_term(): jnp.einsum('jac,jcd->jad', inner, right_env[index], preferred_element_typ...  16.2 us
    another operation x3, other arithmetic, finish_basis(): lower = jnp.linalg.cholesky(gram)  12.4 us
    another operation x1, loops' own time, body(): lax.fori_loop(0, t_dev, one_term, jnp.zeros((sec_dev, lax.axis_size('op')...  10.6 us
    another operation x2, other arithmetic, finish_basis(): lax.linalg.triangular_solve(lower, sampled, left_side=False, lower=True,...  10.5 us
    ppermute x1, waiting for transfers between devices, padded_2(): lax.ppermute(lax.slice_in_dim(block, block.shape[dim] - width, None, axis...  9.87 us
    ppermute x1, starting transfers between devices, padded_2(): lax.ppermute(lax.slice_in_dim(block, 0, width, axis=dim), axis, backward)  5.81 us
  transfers between devices with their start and end apart: 4, of which 4 were waited for; matrix products, arithmetic and copies ran while one was open for 0% of the time, Pallas kernels for 0%

commit v1 on v0

v1 whole, which is shorter than its diff:
```python
import functools
import math

import jax
import jax.numpy as jnp
from jax import lax
from jax.experimental import pallas as pl
from jax.experimental.pallas import tpu as pltpu
from jax.sharding import PartitionSpec as P

BF = jnp.bfloat16
F32 = jnp.float32


def main_kernel(code, core, psi, near, far, left, right, sketch, mine, other, acc, inner):
    t = pl.program_id(0)
    k = code[t]
    first = jnp.where(core[0] == 0, 2, 0)

    def times(source):
        inner[...] = jnp.dot(left[0, 0], source[...], preferred_element_type=F32).astype(BF)

    pl.when(k == 1)(lambda: times(psi))
    pl.when(k == first)(lambda: times(near))
    pl.when(k == 2 - first)(lambda: times(far))
    part = jnp.dot(inner[...], right[0, 0], preferred_element_type=F32)

    @pl.when(t == 0)
    def _():
        acc[...] = part

    @pl.when(t > 0)
    def _():
        acc[...] += part

    @pl.when(t == pl.num_programs(0) - 1)
    def _():
        c = core[0]
        scale = 1.0 / math.sqrt(128)
        for p in range(8):
            for half, ref in ((c, mine), (1 - c, other)):
                start = pl.multiple_of((2 * p + half) * 32, 32)
                rows = acc[pl.ds(start, 32), :] * scale
                some = jnp.dot(rows.astype(BF), sketch[...], preferred_element_type=F32)
                ref[pl.ds(32 * p, 32), :512] = rows.astype(ref.dtype)
                ref[pl.ds(32 * p, 32), 512:] = some.astype(ref.dtype)


def pack_kernel(mine, got, out):
    for p in range(8):
        rows = pl.ds(32 * p, 32)
        for j in range(4):
            cols = pl.ds(128 * j, 128)
            out[p, 32 * j : 32 * j + 32, :] = (mine[rows, cols] + got[rows, cols].astype(F32)).astype(BF)
    some = (mine[:, 512:] + got[:, 512:].astype(F32)).astype(BF)
    for p in range(8):
        out[p, 128:, :] = some


def sum_kernel(place, got, sigma, half, gram):
    for j in range(4):
        rows = pl.ds(32 * j, 32)
        total = got[0, rows, :].astype(F32)
        for p in range(1, 8):
            total += got[p, rows, :].astype(F32)
        sigma[:, 128 * j : 128 * j + 128] = total.astype(BF)
    total = got[0, 128:, :].astype(F32)
    for p in range(1, 8):
        total += got[p, 128:, :].astype(F32)
    gram[...] = lax.dot_general(
        total, total, (((0,), (0,)), ((), ())), precision=lax.Precision.HIGHEST, preferred_element_type=F32
    )
    half[...] = total


def exchanged(n_op, n_sec):
    pairs = []
    for s in range(n_sec - 1):
        flip = 8 if s == n_sec // 2 - 1 else 0
        for o in range(n_op):
            low, high = (o ^ flip) * n_sec + s, o * n_sec + s + 1
            if o % 2 == 0:
                pairs.append((low, high))
            else:
                pairs.append(((o ^ flip) * n_sec + s + 1, o * n_sec + s))
    return pairs


def body(psi, left_env, right_env, pair_code, sketch):
    terms = left_env.shape[0]
    n_op, n_sec = lax.axis_size("op"), lax.axis_size("sec")
    swap = [(i, i ^ 1) for i in range(n_op)]
    place = lax.axis_index("op")
    core = (place % 2).astype(jnp.int32).reshape(1)
    near = lax.ppermute(psi[0], ("op", "sec"), exchanged(n_op, n_sec))
    far = lax.ppermute(near, "op", swap)
    smem = pl.BlockSpec(memory_space=pltpu.SMEM)
    vmem = pl.BlockSpec(memory_space=pltpu.VMEM)
    big = pl.BlockSpec((1, 1, 512, 512), lambda t: (t, 0, 0, 0))
    mine, other = pl.pallas_call(
        main_kernel,
        grid=(terms,),
        in_specs=[smem, smem, vmem, vmem, vmem, big, big, vmem],
        out_specs=[vmem, vmem],
        out_shape=[jax.ShapeDtypeStruct((256, 640), F32), jax.ShapeDtypeStruct((256, 640), BF)],
        scratch_shapes=[pltpu.VMEM((512, 512), F32), pltpu.VMEM((512, 512), BF)],
        compiler_params=pltpu.CompilerParams(vmem_limit_bytes=24 * 2**20),
        name="main",
    )(pair_code, core, psi[0], near, far, left_env, right_env, sketch[0])
    got = lax.ppermute(other, "op", swap)
    packed = pl.pallas_call(
        pack_kernel,
        in_specs=[vmem, vmem],
        out_specs=vmem,
        out_shape=jax.ShapeDtypeStruct((8, 384, 128), BF),
        name="pack",
    )(mine, got)
    groups = [[2 * p + c for p in range(8)] for c in range(2)]
    parts = lax.all_to_all(packed, "op", 0, 0, axis_index_groups=groups, tiled=True)
    sigma, half, gram = pl.pallas_call(
        sum_kernel,
        in_specs=[smem, vmem],
        out_specs=[vmem, vmem, vmem],
        out_shape=[
            jax.ShapeDtypeStruct((32, 512), BF),
            jax.ShapeDtypeStruct((256, 128), F32),
            jax.ShapeDtypeStruct((128, 128), F32),
        ],
        name="gram",
    )(core, parts)
    gram = gram + lax.ppermute(gram, "op", swap)
    rows = lax.dynamic_slice_in_dim(half, (place // 2) * 32, 32, 0)
    lower = jnp.linalg.cholesky(gram)
    basis = math.sqrt(512) * lax.linalg.triangular_solve(
        lower, rows, left_side=False, lower=True, transpose_a=True
    )
    return sigma, basis


def solution(mesh):
    in_specs = (
        P("sec", None, None),
        P("op", "sec", None, None),
        P("op", "sec", None, None),
        P("op"),
        P("sec", None, None),
    )
    out_specs = (P("op", "sec"), P("op", "sec"))
    return jax.shard_map(body, mesh=mesh, in_specs=in_specs, out_specs=out_specs, check_vma=False)
```

time: 276 us -> 86.8 us (0.31); the launches traced: 273 us -> 86.4 us
  waiting for transfers between devices: 188 us -> 10.1 us
  matrix products: 18 us -> 1.5 us
  blocking collectives: 0 us -> 16.5 us
  between operations: 14.1 us -> 0.71 us
  Pallas kernels: 0 us -> 13.1 us
  loops' own time: 10.6 us -> 0 us
  other arithmetic: 25.9 us -> 22.9 us
  local copies, waits for them, and re-layouts: 6.61 us -> 9.57 us
    psum x1 -> x0, waiting for transfers between devices: 113 us -> none  [body(): gram = lax.psum(gram_part, 'op')]
    reduce_scatter x1 -> x0, waiting for transfers between devices: 63.6 us -> none  [body(): lax.psum_scatter(total.transpose(1, 0, 2).reshape(lax.axis_size('op') * r...]
    dot_general x10 -> x0, matrix products: 17.2 us -> none  [the longest x8 16.2 us: one_term(): jnp.einsum('jac,jcd->jad', inner, right_env[index], preferred_element_typ...]
    all_to_all x0 -> x1, blocking collectives: none -> 16.5 us  [body(): lax.all_to_all(packed, 'op', 0, 0, axis_index_groups=groups, tiled=True)]
    pallas_call x0 -> x3, Pallas kernels: none -> 13.1 us  [the longest x1 8.89 us: body(): pl.pallas_call(main_kernel, grid=(terms,), in_specs=[smem, smem, vmem, vm...]
    another operation x1 -> x0, loops' own time: 10.6 us -> none  [body(): lax.fori_loop(0, t_dev, one_term, jnp.zeros((sec_dev, lax.axis_size('op')...]
    unnamed x8 -> x14, local copies, waits for them, and re-layouts: 0.99 us -> 8.56 us
    dynamic_slice x8 -> x0, local copies, waits for them, and re-layouts: 4.69 us -> none  [one_term(): code = pair_code[index]]
where the time goes in v1:
time: 86.8 us; the launch traced here: 86.4 us
  other arithmetic  22.9 us (26%)
  blocking collectives  16.5 us (19%)
  Pallas kernels  13.1 us (15%)
  starting transfers between devices  12 us (14%)
  waiting for transfers between devices  10.1 us (12%)
  local copies, waits for them, and re-layouts  9.57 us (11%)
  matrix products  1.5 us (2%)
    all_to_all x1, blocking collectives, body(): lax.all_to_all(packed, 'op', 0, 0, axis_index_groups=groups, tiled=True)  16.5 us
    another operation x3, other arithmetic, body(): lower = jnp.linalg.cholesky(gram)  12.4 us
    another operation x2, other arithmetic, body(): lax.linalg.triangular_solve(lower, rows, left_side=False, lower=True, tra...  10.5 us
    pallas_call x1, Pallas kernels, body(): pl.pallas_call(main_kernel, grid=(terms,), in_specs=[smem, smem, vmem, vm...  8.89 us
    unnamed x14, local copies, waits for them, and re-layouts  8.56 us
    ppermute x1, starting transfers between devices, body(): near = lax.ppermute(psi[0], ('op', 'sec'), exchanged(n_op, n_sec))  7.46 us
    ppermute x1, waiting for transfers between devices, body(): near = lax.ppermute(psi[0], ('op', 'sec'), exchanged(n_op, n_sec))  6.42 us
    ppermute x1, starting transfers between devices, body(): gram = gram + lax.ppermute(gram, 'op', swap)  2.25 us
  transfers between devices with their start and end apart: 4, of which 4 were waited for; matrix products, arithmetic and copies ran while one was open for 0% of the time, Pallas kernels for 0%

profile of v1, /device:TPU:5, one launch (start us, length us, event | category | flops | bytes accessed | tf_op | source)
XLA Modules:
  0.0 86.4 jit_solution(6043648982663584035)
XLA Ops:
  0.6 7.5 %collective-permute-start = (bf16[512,512]{1,0:T(8,128)(2,1)}, bf16[512,512]{1,0:T(8,128)(2,1)S(1)}, u32[]{:S(2)}, u32[]{:S(2)}) collective-permute-start(bf16[512,512]{1,0:T(8,128)(2,1)} %bitcast.12), channel_id=1, source_target_pairs={{0,1},{17,16},{32,33},{49,48},{64,65},{81,80},{96,97},{113,112},{1... | collective-permute-start | bytes 1572872 | tf_op jit(solution)/shard_map/ppermute | solution.py:95
  8.1 6.4 %collective-permute-done.near = bf16[512,512]{1,0:T(8,128)(2,1)S(1)} collective-permute-done((bf16[512,512]{1,0:T(8,128)(2,1)}, bf16[512,512]{1,0:T(8,128)(2,1)S(1)}, u32[]{:S(2)}, u32[]{:S(2)}) %collective-permute-start) | collective-permute-done | bytes 524320 | tf_op jit(solution)/shard_map/ppermute | solution.py:95
  14.5 1.9 %collective-permute-start.1 = (bf16[512,512]{1,0:T(8,128)(2,1)S(1)}, bf16[512,512]{1,0:T(8,128)(2,1)S(1)}, u32[]{:S(2)}, u32[]{:S(2)}) collective-permute-start(bf16[512,512]{1,0:T(8,128)(2,1)S(1)} %collective-permute-done.near), channel_id=1, source_target_pairs={{0,16},{16,0},{32,48},{48,32},{64,80},{80,64},{96,112},{112,96},{1... | collective-permute-start | bytes 1572872 | tf_op jit(solution)/shard_map/ppermute | solution.py:96
  16.4 1.5 %collective-permute-done.1.far = bf16[512,512]{1,0:T(8,128)(2,1)S(1)} collective-permute-done((bf16[512,512]{1,0:T(8,128)(2,1)S(1)}, bf16[512,512]{1,0:T(8,128)(2,1)S(1)}, u32[]{:S(2)}, u32[]{:S(2)}) %collective-permute-start.1) | collective-permute-done | bytes 524320 | tf_op jit(solution)/shard_map/ppermute | solution.py:96
  17.9 0.0 copy-start
  17.9 2.2 %copy-done = bf16[8,1,512,512]{3,2,1,0:T(8,128)(2,1)S(1)} copy-done((bf16[8,1,512,512]{3,2,1,0:T(8,128)(2,1)S(1)}, bf16[8,1,512,512]{3,2,1,0:T(8,128)(2,1)}, u32[]{:S(2)}) %copy-start) | copy-done | bytes 4194328
  20.1 0.0 copy-start.1
  20.1 2.2 %copy-done.1 = bf16[8,1,512,512]{3,2,1,0:T(8,128)(2,1)S(1)} copy-done((bf16[8,1,512,512]{3,2,1,0:T(8,128)(2,1)S(1)}, bf16[8,1,512,512]{3,2,1,0:T(8,128)(2,1)}, u32[]{:S(2)}) %copy-start.1) | copy-done | bytes 4194328
  22.3 0.0 copy-start.3
  22.3 1.0 %copy-done.3 = bf16[1,512,512]{2,1,0:T(8,128)(2,1)S(1)} copy-done((bf16[1,512,512]{2,1,0:T(8,128)(2,1)S(1)}, bf16[1,512,512]{2,1,0:T(8,128)(2,1)}, u32[]{:S(2)}) %copy-start.3) | copy-done | bytes 524312
  23.4 0.0 copy-start.4
  23.4 0.9 %copy-done.4 = bf16[1,512,128]{2,1,0:T(8,128)(2,1)S(1)} copy-done((bf16[1,512,128]{2,1,0:T(8,128)(2,1)S(1)}, bf16[1,512,128]{2,1,0:T(8,128)(2,1)}, u32[]{:S(2)}) %copy-start.4) | copy-done | bytes 131096
  24.3 0.0 copy-start.5
  24.3 0.7 copy-done.5
  24.9 8.9 %main.1 = (f32[256,640]{1,0:T(8,128)S(1)}, bf16[256,640]{1,0:T(8,128)(2,1)S(1)}) custom-call(s32[8]{0:T(128)S(1)} %copy-done.5, s32[1]{0:T(128)} %bitcast.core.place, bf16[512,512]{1,0:T(8,128)(2,1)S(1)} %bitcast.13, bf16[512,512]{1,0:T(8,128)(2,1)S(1)} %collective-permute-done.near, bf16[512,512]{1,0:T(8,128)(2,1)S(1)} %collective-permute-done.1.far, ...), custom_call_target="tpu_custom_call" | custom-call | tf_op jit(solution)/shard_map/main/pallas_call | solution.py:100
  33.8 0.0 copy-start.2
  33.8 0.9 copy-done.2
  34.7 0.4 collective-permute-start.2
  35.1 1.3 %collective-permute-done.2.got = bf16[256,640]{1,0:T(8,128)(2,1)S(1)} collective-permute-done((bf16[256,640]{1,0:T(8,128)(2,1)S(1)}, bf16[256,640]{1,0:T(8,128)(2,1)S(1)}, u32[]{:S(2)}, u32[]{:S(2)}) %collective-permute-start.2) | collective-permute-done | bytes 327712 | tf_op jit(solution)/shard_map/ppermute | solution.py:110
  36.3 0.0 copy-start.6
  36.3 0.7 copy-done.6
  37.1 2.1 %pack.1 = bf16[8,384,128]{2,1,0:T(8,128)(2,1)} custom-call(f32[256,640]{1,0:T(8,128)} %copy-done.2, bf16[256,640]{1,0:T(8,128)(2,1)} %copy-done.6), custom_call_target="tpu_custom_call" | custom-call | tf_op jit(solution)/shard_map/pack/pallas_call | solution.py:111
  39.2 16.5 %all_to_all.5.got = bf16[8,384,128]{2,1,0:T(8,128)(2,1)} all-to-all(bf16[8,384,128]{2,1,0:T(8,128)(2,1)} %pack.1), channel_id=1, replica_groups={{0,32,64,96,128,160,192,224},{16,48,80,112,144,176,208,240},{1,33,65,97..., dimensions={0} | all-to-all | bytes 1572864 | tf_op jit(solution)/shard_map/all_to_all | solution.py:119
  55.7 2.1 %gram.1 = (bf16[32,512]{1,0:T(8,128)(2,1)}, f32[256,128]{1,0:T(8,128)}, f32[128,128]{1,0:T(8,128)}) custom-call(s32[1]{0:T(128)} %bitcast.core.place, bf16[8,384,128]{2,1,0:T(8,128)(2,1)} %all_to_all.5.got), custom_call_target="tpu_custom_call" | custom-call | tf_op jit(solution)/shard_map/gram/pallas_call | solution.py:120
  57.8 0.9 %copy.8 = f32[128,128]{0,1:T(8,128)S(1)} copy(f32[128,128]{1,0:T(8,128)} %get-tuple-element.11) | data formatting | bytes 131072 | tf_op jit(solution)/shard_map/gram/pallas_call | solution.py:120
  58.7 2.2 %collective-permute-start.3 = (f32[128,128]{0,1:T(8,128)S(1)}, f32[128,128]{0,1:T(8,128)S(1)}, u32[]{:S(2)}, u32[]{:S(2)}) collective-permute-start(f32[128,128]{0,1:T(8,128)S(1)} %copy.8), channel_id=1, source_target_pairs={{0,16},{16,0},{32,48},{48,32},{64,80},{80,64},{96,112},{112,96},{1... | collective-permute-start | bytes 196616 | tf_op jit(solution)/shard_map/ppermute | solution.py:131
  61.0 0.9 %collective-permute-done.3 = f32[128,128]{0,1:T(8,128)S(1)} collective-permute-done((f32[128,128]{0,1:T(8,128)S(1)}, f32[128,128]{0,1:T(8,128)S(1)}, u32[]{:S(2)}, u32[]{:S(2)}) %collective-permute-start.3) | collective-permute-done | bytes 65568 | tf_op jit(solution)/shard_map/ppermute | solution.py:131
  61.9 0.1 copy.9
  62.0 11.7 %cholesky.16 = f32[128,128]{1,0:T(8,128)S(1)} custom-call(f32[128,128]{1,0:T(8,128)S(1)} %fusion.2), custom_call_target="Cholesky" | custom-call | tf_op jit(solution)/shard_map/jit(cholesky)/cholesky | solution.py:133
  73.7 0.6 compare_reduce_fusion
  74.4 0.7 fusion
  75.0 9.8 %custom-call.6 = f32[1,128,128]{1,2,0:T(8,128)S(1)} custom-call(f32[1,128,128]{2,1,0:T(8,128)S(1)} %fusion), custom_call_target="InvertDiagBlocksLowerTriangular" | custom-call | tf_op jit(solution)/shard_map/triangular_solve | solution.py:134
  84.9 1.5 %convolution_multiply_fusion = f32[32,128]{1,0:T(8,128)} fusion(f32[1,128,128]{1,2,0:T(8,128)S(1)} %custom-call.6, f32[256,128]{1,0:T(8,128)} %get-tuple-element.10, s32[]{:T(128)S(6)} %select_n.20), kind=kOutput, calls=%fused_computation | convolution fusion | flops 6295552 | bytes 98308 | tf_op jit(solution)/shard_map/triangular_solve | solution.py:134
  (3 shorter events, 0.1 us)
Async XLA Ops:
  0.6 13.9 %collective-permute-start = (bf16[512,512]{1,0:T(8,128)(2,1)}, bf16[512,512]{1,0:T(8,128)(2,1)S(1)}, u32[]{:S(2)}, u32[]{:S(2)}) collective-permute-start(bf16[512,512]{1,0:T(8,128)(2,1)} %bitcast.12), channel_id=1, source_target_pairs={{0,1},{17,16},{32,33},{49,48},{64,65},{81,80},{96,97},{113,112},{1... | collective-permute-start | bytes 1572872 | tf_op jit(solution)/shard_map/ppermute | solution.py:95
  14.5 3.4 %collective-permute-start.1 = (bf16[512,512]{1,0:T(8,128)(2,1)S(1)}, bf16[512,512]{1,0:T(8,128)(2,1)S(1)}, u32[]{:S(2)}, u32[]{:S(2)}) collective-permute-start(bf16[512,512]{1,0:T(8,128)(2,1)S(1)} %collective-permute-done.near), channel_id=1, source_target_pairs={{0,16},{16,0},{32,48},{48,32},{64,80},{80,64},{96,112},{112,96},{1... | collective-permute-start | bytes 1572872 | tf_op jit(solution)/shard_map/ppermute | solution.py:96
  17.9 2.2 %copy-start = (bf16[8,1,512,512]{3,2,1,0:T(8,128)(2,1)S(1)}, bf16[8,1,512,512]{3,2,1,0:T(8,128)(2,1)}, u32[]{:S(2)}) copy-start(bf16[8,1,512,512]{3,2,1,0:T(8,128)(2,1)} %left.1) | copy-start | bytes 12582916
  20.1 2.2 %copy-start.1 = (bf16[8,1,512,512]{3,2,1,0:T(8,128)(2,1)S(1)}, bf16[8,1,512,512]{3,2,1,0:T(8,128)(2,1)}, u32[]{:S(2)}) copy-start(bf16[8,1,512,512]{3,2,1,0:T(8,128)(2,1)} %right.1) | copy-start | bytes 12582916
  22.3 1.0 %copy-start.3 = (bf16[1,512,512]{2,1,0:T(8,128)(2,1)S(1)}, bf16[1,512,512]{2,1,0:T(8,128)(2,1)}, u32[]{:S(2)}) copy-start(bf16[1,512,512]{2,1,0:T(8,128)(2,1)} %param.5) | copy-start | bytes 1572868
  23.4 0.9 %copy-start.4 = (bf16[1,512,128]{2,1,0:T(8,128)(2,1)S(1)}, bf16[1,512,128]{2,1,0:T(8,128)(2,1)}, u32[]{:S(2)}) copy-start(bf16[1,512,128]{2,1,0:T(8,128)(2,1)} %param.9) | copy-start | bytes 393220
  24.3 0.7 copy-start.5
  33.8 0.9 %copy-start.2 = (f32[256,640]{1,0:T(8,128)}, f32[256,640]{1,0:T(8,128)S(1)}, u32[]{:S(2)}) copy-start(f32[256,640]{1,0:T(8,128)S(1)} %get-tuple-element.7.mine) | copy-start | bytes 1966084
  34.7 1.6 %collective-permute-start.2 = (bf16[256,640]{1,0:T(8,128)(2,1)S(1)}, bf16[256,640]{1,0:T(8,128)(2,1)S(1)}, u32[]{:S(2)}, u32[]{:S(2)}) collective-permute-start(bf16[256,640]{1,0:T(8,128)(2,1)S(1)} %get-tuple-element.8), channel_id=1, source_target_pairs={{0,16},{16,0},{32,48},{48,32},{64,80},{80,64},{96,112},{112,96},{1... | collective-permute-start | bytes 983048 | tf_op jit(solution)/shard_map/ppermute | solution.py:110
  36.3 0.7 copy-start.6
  58.7 3.2 %collective-permute-start.3 = (f32[128,128]{0,1:T(8,128)S(1)}, f32[128,128]{0,1:T(8,128)S(1)}, u32[]{:S(2)}, u32[]{:S(2)}) collective-permute-start(f32[128,128]{0,1:T(8,128)S(1)} %copy.8), channel_id=1, source_target_pairs={{0,16},{16,0},{32,48},{48,32},{64,80},{80,64},{96,112},{112,96},{1... | collective-permute-start | bytes 196616 | tf_op jit(solution)/shard_map/ppermute | solution.py:131

commit v2 on v1

v2 whole, which is shorter than its diff:
```python
import functools
import math

import jax
import jax.numpy as jnp
from jax import lax
from jax.experimental import pallas as pl
from jax.experimental.pallas import tpu as pltpu
from jax.sharding import PartitionSpec as P

BF = jnp.bfloat16
F32 = jnp.float32
EXACT = lax.Precision.HIGHEST
HBM = pl.BlockSpec(memory_space=pltpu.HBM)
VMEM = pl.BlockSpec(memory_space=pltpu.VMEM)
SMEM = pl.BlockSpec(memory_space=pltpu.SMEM)
MIB = 2**20


def call(kernel, name, in_specs, outs, scratch=(), limit=8, flops=1000, bytes_accessed=1000):
    return pl.pallas_call(
        kernel,
        in_specs=in_specs,
        out_specs=[VMEM] * len(outs),
        out_shape=[jax.ShapeDtypeStruct(shape, dtype) for shape, dtype in outs],
        scratch_shapes=scratch,
        compiler_params=pltpu.CompilerParams(vmem_limit_bytes=limit * MIB),
        cost_estimate=pl.CostEstimate(flops=flops, bytes_accessed=bytes_accessed, transcendentals=0),
        name=name,
    )


def load_kernel(left, right, psi, sketch, lout, rout, pout, sout, sems):
    core = lax.axis_index("op") % 2
    copies = [
        pltpu.make_async_copy(psi, pout, sems.at[0]),
        pltpu.make_async_copy(sketch, sout, sems.at[1]),
        pltpu.make_async_copy(left.at[:, :, core], lout.at[:, 0], sems.at[2]),
        pltpu.make_async_copy(left.at[:, :, 1 - core], lout.at[:, 1], sems.at[3]),
        pltpu.make_async_copy(right, rout, sems.at[4]),
    ]
    for copy in copies:
        copy.start()
    for copy in copies:
        copy.wait()


def main_kernel(code, psi, near, far, left, right, sketch, mine, other, inner):
    core = lax.axis_index("op") % 2
    first = jnp.where(core == 0, 2, 0)
    terms = left.shape[0]
    for t in range(terms):
        k = code[t]
        rows = left[t].reshape(512, 512)
        cols = pl.ds(512 * t, 512)

        def times(source):
            inner[:, cols] = jnp.dot(rows, source[...], preferred_element_type=F32).astype(BF)

        pl.when(k == 1)(lambda: times(psi))
        pl.when(k == first)(lambda: times(near))
        pl.when(k == 2 - first)(lambda: times(far))
    scale = 1.0 / math.sqrt(128)
    for h, ref in ((1, other), (0, mine)):
        total = scale * jnp.dot(inner[256 * h : 256 * h + 256, :], right[...], preferred_element_type=F32)
        some = jnp.dot(total.astype(BF), sketch[...], preferred_element_type=F32)
        ref[:, :512] = total.astype(ref.dtype)
        ref[:, 512:] = some.astype(ref.dtype)


def pack_kernel(mine, got, out):
    for p in range(8):
        rows = pl.ds(32 * p, 32)
        for j in range(4):
            cols = pl.ds(128 * j, 128)
            out[p, 32 * j : 32 * j + 32, :] = (mine[rows, cols] + got[rows, cols].astype(F32)).astype(BF)
    some = (mine[:, 512:] + got[:, 512:].astype(F32)).astype(BF)
    for p in range(8):
        out[p, 128:, :] = some


def sum_kernel(got, sigma, half, gram):
    for j in range(4):
        rows = pl.ds(32 * j, 32)
        total = got[0, rows, :].astype(F32)
        for p in range(1, 8):
            total += got[p, rows, :].astype(F32)
        sigma[:, 128 * j : 128 * j + 128] = total.astype(BF)
    total = got[0, 128:, :].astype(F32)
    for p in range(1, 8):
        total += got[p, 128:, :].astype(F32)
    gram[...] = lax.dot_general(
        total, total, (((0,), (0,)), ((), ())), precision=EXACT, preferred_element_type=F32
    )
    half[...] = total


def inverse_rows(a, w, ahead):
    n = len(a)
    row = lax.broadcasted_iota(jnp.int32, (8, 128), 0)
    out = []
    for b in range(n):
        near = range(b, min(b + 1 + ahead, n))
        c = {v: [jnp.broadcast_to(a[v][:, 8 * b + k : 8 * b + k + 1], (8, 128)) for k in range(8)] for v in near}
        scale = jnp.zeros((8, 128), F32)
        for k in range(8):
            s = lax.rsqrt(jnp.broadcast_to(c[b][k][k : k + 1, :], (8, 128)))
            scale = jnp.where(row == k, s, scale)
            f = {v: c[v][k] * (s * s) for v in near}
            f[b] = jnp.where(row > k, f[b], 0.0)
            for m in range(k + 1, 8):
                q = jnp.broadcast_to(c[b][m][k : k + 1, :], (8, 128))
                for v in near:
                    c[v][m] = c[v][m] - f[v] * q
            pa = jnp.broadcast_to(a[b][k : k + 1, :], (8, 128))
            pw = jnp.broadcast_to(w[b][k : k + 1, :], (8, 128))
            for v in near:
                a[v] = a[v] - f[v] * pa
                w[v] = w[v] - f[v] * pw
        u, z = a[b] * scale, w[b] * scale
        out.append(z)
        if b + 1 + ahead < n:
            step = lax.dot_general(
                u, jnp.concatenate([u, z], 1), (((0,), (0,)), ((), ())), precision=EXACT, preferred_element_type=F32
            )
            for v in range(b + 1 + ahead, n):
                a[v] = a[v] - step[8 * v : 8 * v + 8, :128]
                w[v] = w[v] - step[8 * v : 8 * v + 8, 128:]
    return out


def basis_kernel(gram, got, half, basis):
    place = lax.axis_index("op") // 2
    row = lax.broadcasted_iota(jnp.int32, (8, 128), 0)
    lane = lax.broadcasted_iota(jnp.int32, (8, 128), 1)
    a = [gram[8 * v : 8 * v + 8, :] + got[8 * v : 8 * v + 8, :] for v in range(16)]
    w = [jnp.where(lane == row + 8 * v, 1.0, 0.0).astype(F32) for v in range(16)]
    inverse = jnp.concatenate(inverse_rows(a, w, 4), 0)
    rows = half[pl.ds(pl.multiple_of(place * 32, 32), 32), :]
    basis[...] = math.sqrt(512) * lax.dot_general(
        rows, inverse, (((1,), (1,)), ((), ())), precision=EXACT, preferred_element_type=F32
    )


def exchanged(n_op, n_sec):
    pairs = []
    for s in range(n_sec - 1):
        flip = 8 if s == n_sec // 2 - 1 else 0
        for o in range(n_op):
            source, target = (s, s + 1) if o % 2 == 0 else (s + 1, s)
            pairs.append(((o ^ flip) * n_sec + source, o * n_sec + target))
    return pairs


def body(psi, left_env, right_env, pair_code, sketch):
    terms = left_env.shape[0]
    n_op, n_sec = lax.axis_size("op"), lax.axis_size("sec")
    swap = [(i, i ^ 1) for i in range(n_op)]
    near = lax.ppermute(psi[0], ("op", "sec"), exchanged(n_op, n_sec))
    hbm = functools.partial(pltpu.with_memory_space_constraint, memory_space=pltpu.HBM)
    left, right, here, sketch = call(
        load_kernel,
        "load",
        [HBM] * 4,
        [((terms, 2, 8, 32, 512), BF), ((terms * 512, 512), BF), ((512, 512), BF), ((512, 128), BF)],
        [pltpu.SemaphoreType.DMA((5,))],
        limit=1,
        bytes_accessed=18 * MIB,
    )(
        hbm(left_env.reshape(terms, 8, 2, 32, 512)),
        hbm(right_env.reshape(terms * 512, 512)),
        hbm(psi[0]),
        hbm(sketch[0]),
    )
    near, left, right, here, sketch = lax.optimization_barrier((near, left, right, here, sketch))
    far = lax.ppermute(near, "op", swap)
    mine, other = call(
        main_kernel,
        "main",
        [SMEM] + [VMEM] * 6,
        [((256, 640), F32), ((256, 640), BF)],
        [pltpu.VMEM((512, 512 * terms), BF)],
        limit=16,
        flops=4 * 512**3 * terms,
    )(pair_code, here, near, far, left, right, sketch)
    got = lax.ppermute(other, "op", swap)
    (packed,) = call(pack_kernel, "pack", [VMEM] * 2, [((8, 384, 128), BF)])(mine, got)
    groups = [[2 * p + c for p in range(8)] for c in range(2)]
    parts = lax.all_to_all(packed, "op", 0, 0, axis_index_groups=groups, tiled=True)
    sigma, half, gram = call(
        sum_kernel, "gram", [VMEM], [((32, 512), BF), ((256, 128), F32), ((128, 128), F32)]
    )(parts)
    (basis,) = call(basis_kernel, "basis", [VMEM] * 3, [((32, 128), F32)])(
        gram, lax.ppermute(gram, "op", swap), half
    )
    return sigma, basis


def solution(mesh):
    in_specs = (
        P("sec", None, None),
        P("op", "sec", None, None),
        P("op", "sec", None, None),
        P("op"),
        P("sec", None, None),
    )
    out_specs = (P("op", "sec"), P("op", "sec"))
    return jax.shard_map(body, mesh=mesh, in_specs=in_specs, out_specs=out_specs, check_vma=False)
```

time: 86.8 us -> 52.1 us (0.60)
  other arithmetic: 22.9 us -> 0 us
  local copies, waits for them, and re-layouts: 9.57 us -> 0.01 us
  waiting for transfers between devices: 10.1 us -> 6.38 us
  Pallas kernels: 13.1 us -> 16.7 us
  matrix products: 1.5 us -> 0 us
    another operation x5 -> x0, other arithmetic: 22.9 us -> none  [the longest x3 12.4 us: body(): lower = jnp.linalg.cholesky(gram)]
    unnamed x14 -> x2, local copies, waits for them, and re-layouts: 8.56 us -> 0.01 us
    ppermute x1, waiting for transfers between devices: 6.42 us -> 2.68 us  [body(): near = lax.ppermute(psi[0], ('op', 'sec'), exchanged(n_op, n_sec))]
    pallas_call x3 -> x5, Pallas kernels: 13.1 us -> 16.7 us  [the longest x1 6.9 us: body(): call(main_kernel, 'main', [SMEM] + [VMEM] * 6, [((256, 640), F32), ((256,...]
    another operation x1 -> x0, matrix products: 1.5 us -> none  [body(): lax.linalg.triangular_solve(lower, rows, left_side=False, lower=True, tra...]
    pallas_call x1 -> x0, local copies, waits for them, and re-layouts: 0.93 us -> none  [body(): pl.pallas_call(sum_kernel, in_specs=[smem, vmem], out_specs=[vmem, vmem,...]
  transfers between devices with their start and end apart: 4 -> 4, of which waited for: 4 -> 4; matrix products, arithmetic and copies ran while one was open for 0% -> 0% of each run, Pallas kernels for 0% -> 7%
where the time goes in v2:
time: 52.1 us; the launch traced here: 51.9 us
  Pallas kernels  16.7 us (32%)
  blocking collectives  16.2 us (31%)
  starting transfers between devices  12 us (23%)
  waiting for transfers between devices  6.38 us (12%)
  between operations  0.67 us (1%)
    all_to_all x1, blocking collectives, body(): lax.all_to_all(packed, 'op', 0, 0, axis_index_groups=groups, tiled=True)  16.2 us
    ppermute x1, starting transfers between devices, body(): near = lax.ppermute(psi[0], ('op', 'sec'), exchanged(n_op, n_sec))  7.46 us
    pallas_call x1, Pallas kernels, body(): call(main_kernel, 'main', [SMEM] + [VMEM] * 6, [((256, 640), F32), ((256,...  6.9 us
    pallas_call x1, Pallas kernels, body(): call(basis_kernel, 'basis', [VMEM] * 3, [((32, 128), F32)])  5.03 us
    pallas_call x1, Pallas kernels, body(): call(load_kernel, 'load', [HBM] * 4, [((terms, 2, 8, 32, 512), BF), ((ter...  3.72 us
    ppermute x1, waiting for transfers between devices, body(): near = lax.ppermute(psi[0], ('op', 'sec'), exchanged(n_op, n_sec))  2.68 us
    ppermute x1, starting transfers between devices, body(): lax.ppermute(gram, 'op', swap)  2.16 us
    ppermute x1, starting transfers between devices, body(): far = lax.ppermute(near, 'op', swap)  1.89 us
  transfers between devices with their start and end apart: 4, of which 4 were waited for; matrix products, arithmetic and copies ran while one was open for 0% of the time, Pallas kernels for 7%

profile of v2, /device:TPU:5, one launch (start us, length us, event | category | flops | bytes accessed | tf_op | source)
XLA Modules:
  0.0 51.9 jit_solution(4608299786657202568)
XLA Ops:
  0.6 7.5 %collective-permute-start = (bf16[512,512]{1,0:T(8,128)(2,1)}, bf16[512,512]{1,0:T(8,128)(2,1)S(1)}, u32[]{:S(2)}, u32[]{:S(2)}) collective-permute-start(bf16[512,512]{1,0:T(8,128)(2,1)} %bitcast.6), channel_id=1, source_target_pairs={{0,1},{17,16},{32,33},{49,48},{64,65},{81,80},{96,97},{113,112},{1... | collective-permute-start | bytes 1572872 | tf_op jit(solution)/shard_map/ppermute | solution.py:159
  8.1 0.0 copy-start
  8.1 3.7 %load.1 = (bf16[8,2,8,32,512]{4,3,2,1,0:T(8,128)(2,1)S(1)}, bf16[4096,512]{1,0:T(8,128)(2,1)S(1)}, bf16[512,512]{1,0:T(8,128)(2,1)S(1)}, bf16[512,128]{1,0:T(8,128)(2,1)S(1)}) custom-call(bf16[8,8,2,32,512]{4,3,2,1,0:T(8,128)(2,1)} %bitcast.4, bf16[4096,512]{1,0:T(8,128)(2,1)} %bitcast.5, bf16[512,512]{1,0:T(8,128)(2,1)} %bitcast.7, bf16[512,128]{1,0:T(8,128)(2,1)} %bitcast.8), custom_call_target="tpu_custom_call" | custom-call | flops 1000 | bytes 18874368 | tf_op jit(solution)/shard_map/load/pallas_call | solution.py:161
  11.8 2.7 %collective-permute-done.near = bf16[512,512]{1,0:T(8,128)(2,1)S(1)} collective-permute-done((bf16[512,512]{1,0:T(8,128)(2,1)}, bf16[512,512]{1,0:T(8,128)(2,1)S(1)}, u32[]{:S(2)}, u32[]{:S(2)}) %collective-permute-start) | collective-permute-done | bytes 524320 | tf_op jit(solution)/shard_map/ppermute | solution.py:159
  14.5 1.9 %collective-permute-start.1 = (bf16[512,512]{1,0:T(8,128)(2,1)S(1)}, bf16[512,512]{1,0:T(8,128)(2,1)S(1)}, u32[]{:S(2)}, u32[]{:S(2)}) collective-permute-start(bf16[512,512]{1,0:T(8,128)(2,1)S(1)} %collective-permute-done.near), channel_id=1, source_target_pairs={{0,16},{16,0},{32,48},{48,32},{64,80},{80,64},{96,112},{112,96},{1... | collective-permute-start | bytes 1572872 | tf_op jit(solution)/shard_map/ppermute | solution.py:176
  16.4 1.5 %collective-permute-done.1.far = bf16[512,512]{1,0:T(8,128)(2,1)S(1)} collective-permute-done((bf16[512,512]{1,0:T(8,128)(2,1)S(1)}, bf16[512,512]{1,0:T(8,128)(2,1)S(1)}, u32[]{:S(2)}, u32[]{:S(2)}) %collective-permute-start.1) | collective-permute-done | bytes 524320 | tf_op jit(solution)/shard_map/ppermute | solution.py:176
  17.9 0.0 copy-done
  17.9 6.9 %main.1 = (f32[256,640]{1,0:T(8,128)S(1)}, bf16[256,640]{1,0:T(8,128)(2,1)S(1)}) custom-call(s32[8]{0:T(128)S(1)} %copy-done, bf16[512,512]{1,0:T(8,128)(2,1)S(1)} %get-tuple-element.20.psi, bf16[512,512]{1,0:T(8,128)(2,1)S(1)} %collective-permute-done.near, bf16[512,512]{1,0:T(8,128)(2,1)S(1)} %collective-permute-done.1.far, ...), custom_call_target="tpu_custom_call" | custom-call | flops 4294967296 | bytes 1000 | tf_op jit(solution)/shard_map/main/pallas_call | solution.py:177
  24.9 0.4 collective-permute-start.2
  25.3 1.3 %collective-permute-done.2.got = bf16[256,640]{1,0:T(8,128)(2,1)S(1)} collective-permute-done((bf16[256,640]{1,0:T(8,128)(2,1)S(1)}, bf16[256,640]{1,0:T(8,128)(2,1)S(1)}, u32[]{:S(2)}, u32[]{:S(2)}) %collective-permute-start.2) | collective-permute-done | bytes 327712 | tf_op jit(solution)/shard_map/ppermute | solution.py:186
  26.6 0.1 pack.1
  26.7 16.2 %all_to_all.5.got = bf16[8,384,128]{2,1,0:T(8,128)(2,1)S(1)} all-to-all(bf16[8,384,128]{2,1,0:T(8,128)(2,1)S(1)} %pack.1), channel_id=1, replica_groups={{0,32,64,96,128,160,192,224},{16,48,80,112,144,176,208,240},{1,33,65,97..., dimensions={0} | all-to-all | bytes 1572864 | tf_op jit(solution)/shard_map/all_to_all | solution.py:189
  42.9 0.9 %gram.1 = (bf16[32,512]{1,0:T(8,128)(2,1)}, f32[256,128]{1,0:T(8,128)S(1)}, f32[128,128]{1,0:T(8,128)S(1)}) custom-call(bf16[8,384,128]{2,1,0:T(8,128)(2,1)S(1)} %all_to_all.5.got), custom_call_target="tpu_custom_call" | custom-call | flops 1000 | bytes 1000 | tf_op jit(solution)/shard_map/gram/pallas_call | solution.py:190
  43.8 2.2 %collective-permute-start.3 = (f32[128,128]{1,0:T(8,128)S(1)}, f32[128,128]{1,0:T(8,128)S(1)}, u32[]{:S(2)}, u32[]{:S(2)}) collective-permute-start(f32[128,128]{1,0:T(8,128)S(1)} %get-tuple-element.28.gram), channel_id=1, source_target_pairs={{0,16},{16,0},{32,48},{48,32},{64,80},{80,64},{96,112},{112,96},{1... | collective-permute-start | bytes 196616 | tf_op jit(solution)/shard_map/ppermute | solution.py:194
  46.0 0.9 %collective-permute-done.3.got = f32[128,128]{1,0:T(8,128)S(1)} collective-permute-done((f32[128,128]{1,0:T(8,128)S(1)}, f32[128,128]{1,0:T(8,128)S(1)}, u32[]{:S(2)}, u32[]{:S(2)}) %collective-permute-start.3) | collective-permute-done | bytes 65568 | tf_op jit(solution)/shard_map/ppermute | solution.py:194
  46.9 5.0 %basis.1 = f32[32,128]{1,0:T(8,128)} custom-call(f32[128,128]{1,0:T(8,128)S(1)} %get-tuple-element.28.gram, f32[128,128]{1,0:T(8,128)S(1)} %collective-permute-done.3.got, f32[256,128]{1,0:T(8,128)S(1)} %get-tuple-element.29.half), custom_call_target="tpu_custom_call" | custom-call | flops 1000 | bytes 1000 | tf_op jit(solution)/shard_map/basis/pallas_call | solution.py:193
Async XLA Ops:
  0.6 13.9 %collective-permute-start = (bf16[512,512]{1,0:T(8,128)(2,1)}, bf16[512,512]{1,0:T(8,128)(2,1)S(1)}, u32[]{:S(2)}, u32[]{:S(2)}) collective-permute-start(bf16[512,512]{1,0:T(8,128)(2,1)} %bitcast.6), channel_id=1, source_target_pairs={{0,1},{17,16},{32,33},{49,48},{64,65},{81,80},{96,97},{113,112},{1... | collective-permute-start | bytes 1572872 | tf_op jit(solution)/shard_map/ppermute | solution.py:159
  8.1 9.9 %copy-start = (s32[8]{0:T(128)S(1)}, s32[8]{0:T(128)}, u32[]{:S(2)}) copy-start(s32[8]{0:T(128)} %code.1) | copy-start | bytes 100
  14.5 3.4 %collective-permute-start.1 = (bf16[512,512]{1,0:T(8,128)(2,1)S(1)}, bf16[512,512]{1,0:T(8,128)(2,1)S(1)}, u32[]{:S(2)}, u32[]{:S(2)}) collective-permute-start(bf16[512,512]{1,0:T(8,128)(2,1)S(1)} %collective-permute-done.near), channel_id=1, source_target_pairs={{0,16},{16,0},{32,48},{48,32},{64,80},{80,64},{96,112},{112,96},{1... | collective-permute-start | bytes 1572872 | tf_op jit(solution)/shard_map/ppermute | solution.py:176
  24.9 1.7 %collective-permute-start.2 = (bf16[256,640]{1,0:T(8,128)(2,1)S(1)}, bf16[256,640]{1,0:T(8,128)(2,1)S(1)}, u32[]{:S(2)}, u32[]{:S(2)}) collective-permute-start(bf16[256,640]{1,0:T(8,128)(2,1)S(1)} %get-tuple-element.26), channel_id=1, source_target_pairs={{0,16},{16,0},{32,48},{48,32},{64,80},{80,64},{96,112},{112,96},{1... | collective-permute-start | bytes 983048 | tf_op jit(solution)/shard_map/ppermute | solution.py:186
  43.8 3.1 %collective-permute-start.3 = (f32[128,128]{1,0:T(8,128)S(1)}, f32[128,128]{1,0:T(8,128)S(1)}, u32[]{:S(2)}, u32[]{:S(2)}) collective-permute-start(f32[128,128]{1,0:T(8,128)S(1)} %get-tuple-element.28.gram), channel_id=1, source_target_pairs={{0,16},{16,0},{32,48},{48,32},{64,80},{80,64},{96,112},{112,96},{1... | collective-permute-start | bytes 196616 | tf_op jit(solution)/shard_map/ppermute | solution.py:194

commit v3 on v2

--- a/solution.py
+++ b/solution.py
@@ -17,55 +17,85 @@
 MIB = 2**20
 
 
-def call(kernel, name, in_specs, outs, scratch=(), limit=8, flops=1000, bytes_accessed=1000):
+def call(kernel, name, in_specs, outs, scratch=(), limit=8, flops=1000, bytes_accessed=1000, aliases={}):
     return pl.pallas_call(
         kernel,
         in_specs=in_specs,
         out_specs=[VMEM] * len(outs),
         out_shape=[jax.ShapeDtypeStruct(shape, dtype) for shape, dtype in outs],
         scratch_shapes=scratch,
+        input_output_aliases=aliases,
         compiler_params=pltpu.CompilerParams(vmem_limit_bytes=limit * MIB),
         cost_estimate=pl.CostEstimate(flops=flops, bytes_accessed=bytes_accessed, transcendentals=0),
         name=name,
     )
 
 
-def load_kernel(left, right, psi, sketch, lout, rout, pout, sout, sems):
+def times(inner, left, t, source):
+    rows = left[t].reshape(512, 512)
+    inner[:, 512 * t : 512 * t + 512] = jnp.dot(rows, source[...], preferred_element_type=F32).astype(BF)
+
+
+def load_kernel(code, left, right, psi, sketch, lout, rout, sout, inner, here, sems):
     core = lax.axis_index("op") % 2
+    sec, last = lax.axis_index("sec"), lax.axis_size("sec") - 1
     copies = [
-        pltpu.make_async_copy(psi, pout, sems.at[0]),
-        pltpu.make_async_copy(sketch, sout, sems.at[1]),
-        pltpu.make_async_copy(left.at[:, :, core], lout.at[:, 0], sems.at[2]),
-        pltpu.make_async_copy(left.at[:, :, 1 - core], lout.at[:, 1], sems.at[3]),
-        pltpu.make_async_copy(right, rout, sems.at[4]),
+        pltpu.make_async_copy(psi, here, sems.at[0]),
+        pltpu.make_async_copy(left.at[:, :, core], lout.at[:, 0], sems.at[1]),
+        pltpu.make_async_copy(left.at[:, :, 1 - core], lout.at[:, 1], sems.at[2]),
+        pltpu.make_async_copy(right, rout, sems.at[3]),
+        pltpu.make_async_copy(sketch, sout, sems.at[4]),
     ]
     for copy in copies:
         copy.start()
-    for copy in copies:
+    for copy in copies[:3]:
         copy.wait()
-
-
-def main_kernel(code, psi, near, far, left, right, sketch, mine, other, inner):
+    for t in range(left.shape[0]):
+        k = code[t]
+
+        @pl.when(k == 1)
+        def _():
+            times(inner, lout, t, here)
+
+        @pl.when(((k == 2) & (sec == 0)) | ((k == 0) & (sec == last)))
+        def _():
+            inner[:, 512 * t : 512 * t + 512] = jnp.zeros((512, 512), BF)
+
+    for copy in copies[3:]:
+        copy.wait()
+
+
+def multiply(code, inner, left, source, wanted):
+    sec, last = lax.axis_index("sec"), lax.axis_size("sec") - 1
+    for t in range(left.shape[0]):
+        k = code[t]
+        empty = ((k == 2) & (sec == 0)) | ((k == 0) & (sec == last))
+
+        @pl.when((k == wanted) & jnp.logical_not(empty))
+        def _():
+            times(inner, left, t, source)
+
+
+def near_kernel(code, near, left, before, inner):
     core = lax.axis_index("op") % 2
-    first = jnp.where(core == 0, 2, 0)
-    terms = left.shape[0]
-    for t in range(terms):
-        k = code[t]
-        rows = left[t].reshape(512, 512)
-        cols = pl.ds(512 * t, 512)
-
-        def times(source):
-            inner[:, cols] = jnp.dot(rows, source[...], preferred_element_type=F32).astype(BF)
-
-        pl.when(k == 1)(lambda: times(psi))
-        pl.when(k == first)(lambda: times(near))
-        pl.when(k == 2 - first)(lambda: times(far))
-    scale = 1.0 / math.sqrt(128)
-    for h, ref in ((1, other), (0, mine)):
-        total = scale * jnp.dot(inner[256 * h : 256 * h + 256, :], right[...], preferred_element_type=F32)
-        some = jnp.dot(total.astype(BF), sketch[...], preferred_element_type=F32)
-        ref[:, :512] = total.astype(ref.dtype)
-        ref[:, 512:] = some.astype(ref.dtype)
+    multiply(code, inner, left, near, jnp.where(core == 0, 2, 0))
+
+
+def finish(inner, right, sketch, h, ref):
+    total = jnp.dot(inner[256 * h : 256 * h + 256, :], right[...], preferred_element_type=F32)
+    total = total * (1.0 / math.sqrt(128))
+    ref[:, :512] = total.astype(ref.dtype)
+    ref[:, 512:] = jnp.dot(total.astype(BF), sketch[...], preferred_element_type=F32).astype(ref.dtype)
+
+
+def far_kernel(code, far, left, right, sketch, before, inner, other):
+    core = lax.axis_index("op") % 2
+    multiply(code, inner, left, far, jnp.where(core == 0, 0, 2))
+    finish(inner, right, sketch, 1, other)
+
+
+def mine_kernel(inner, right, sketch, mine):
+    finish(inner, right, sketch, 0, mine)
 
 
 def pack_kernel(mine, got, out):
@@ -149,6 +179,9 @@
         for o in range(n_op):
             source, target = (s, s + 1) if o % 2 == 0 else (s + 1, s)
             pairs.append(((o ^ flip) * n_sec + source, o * n_sec + target))
+    for o in range(0, n_op, 2):
+        pairs.append((o * n_sec + n_sec - 1, (o + 1) * n_sec + n_sec - 1))
+        pairs.append(((o + 1) * n_sec, o * n_sec))
     return pairs
 
 
@@ -158,32 +191,41 @@
     swap = [(i, i ^ 1) for i in range(n_op)]
     near = lax.ppermute(psi[0], ("op", "sec"), exchanged(n_op, n_sec))
     hbm = functools.partial(pltpu.with_memory_space_constraint, memory_space=pltpu.HBM)
-    left, right, here, sketch = call(
+    products = ((512, 512 * terms), BF)
+    left, right, sketch, inner = call(
         load_kernel,
         "load",
-        [HBM] * 4,
-        [((terms, 2, 8, 32, 512), BF), ((terms * 512, 512), BF), ((512, 512), BF), ((512, 128), BF)],
-        [pltpu.SemaphoreType.DMA((5,))],
-        limit=1,
+        [SMEM] + [HBM] * 4,
+        [((terms, 2, 8, 32, 512), BF), ((terms * 512, 512), BF), ((512, 128), BF), products],
+        [pltpu.VMEM((512, 512), BF), pltpu.SemaphoreType.DMA((5,))],
+        limit=4,
         bytes_accessed=18 * MIB,
     )(
+        pair_code,
         hbm(left_env.reshape(terms, 8, 2, 32, 512)),
         hbm(right_env.reshape(terms * 512, 512)),
         hbm(psi[0]),
         hbm(sketch[0]),
     )
-    near, left, right, here, sketch = lax.optimization_barrier((near, left, right, here, sketch))
+    near, left, right, sketch, inner = lax.optimization_barrier((near, left, right, sketch, inner))
     far = lax.ppermute(near, "op", swap)
-    mine, other = call(
-        main_kernel,
-        "main",
-        [SMEM] + [VMEM] * 6,
-        [((256, 640), F32), ((256, 640), BF)],
-        [pltpu.VMEM((512, 512 * terms), BF)],
-        limit=16,
-        flops=4 * 512**3 * terms,
-    )(pair_code, here, near, far, left, right, sketch)
+    flops = 2 * 512**3 * terms
+    (inner,) = call(
+        near_kernel, "near", [SMEM] + [VMEM] * 3, [products], limit=4, flops=flops // 3, aliases={3: 0}
+    )(pair_code, near, left, inner)
+    inner, other = call(
+        far_kernel,
+        "far",
+        [SMEM] + [VMEM] * 5,
+        [products, ((256, 640), BF)],
+        limit=6,
+        flops=flops,
+        aliases={5: 0},
+    )(pair_code, far, left, right, sketch, inner)
     got = lax.ppermute(other, "op", swap)
+    (mine,) = call(mine_kernel, "mine", [VMEM] * 3, [((256, 640), F32)], limit=6, flops=flops // 2)(
+        inner, right, sketch
+    )
     (packed,) = call(pack_kernel, "pack", [VMEM] * 2, [((8, 384, 128), BF)])(mine, got)
     groups = [[2 * p + c for p in range(8)] for c in range(2)]
     parts = lax.all_to_all(packed, "op", 0, 0, axis_index_groups=groups, tiled=True)

time: 52.1 us -> 47.5 us (0.912)
  waiting for transfers between devices: 6.38 us -> 2.28 us
  starting transfers between devices: 12 us -> 10.7 us
  local copies, waits for them, and re-layouts: 0.01 us -> 0.66 us
  blocking collectives: 16.2 us -> 16.8 us
    ppermute x1, starting transfers between devices: 7.46 us -> 5.63 us  [body(): near = lax.ppermute(psi[0], ('op', 'sec'), exchanged(n_op, n_sec))]
    ppermute x1, waiting for transfers between devices: 1.54 us -> 0.01 us  [body(): far = lax.ppermute(near, 'op', swap)]
    ppermute x1, waiting for transfers between devices: 2.68 us -> 1.38 us  [body(): near = lax.ppermute(psi[0], ('op', 'sec'), exchanged(n_op, n_sec))]
    ppermute x1, waiting for transfers between devices: 1.27 us -> 0.01 us  [body(): got = lax.ppermute(other, 'op', swap)]
    unnamed x2 -> x4, local copies, waits for them, and re-layouts: 0.01 us -> 0.66 us
    all_to_all x1, blocking collectives: 16.2 us -> 16.8 us  [body(): lax.all_to_all(packed, 'op', 0, 0, axis_index_groups=groups, tiled=True)]
    pallas_call x2 -> x4, Pallas kernels: 10.6 us -> 10.6 us  [the longest x1 4.4 us: body(): call(load_kernel, 'load', [SMEM] + [HBM] * 4, [((terms, 2, 8, 32, 512), B...]
  transfers between devices with their start and end apart: 4 -> 4, of which waited for: 4 -> 2; matrix products, arithmetic and copies ran while one was open for 0% -> 0% of each run, Pallas kernels for 7% -> 16%
where the time goes in v3:
time: 47.5 us; the launch traced here: 47.8 us
  blocking collectives  16.8 us (35%)
  Pallas kernels  16.6 us (35%)
  starting transfers between devices  10.7 us (23%)
  waiting for transfers between devices  2.28 us (5%)
  between operations  0.7 us (1%)
  local copies, waits for them, and re-layouts  0.66 us (1%)
    all_to_all x1, blocking collectives, body(): lax.all_to_all(packed, 'op', 0, 0, axis_index_groups=groups, tiled=True)  16.8 us
    ppermute x1, starting transfers between devices, body(): near = lax.ppermute(psi[0], ('op', 'sec'), exchanged(n_op, n_sec))  5.63 us
    pallas_call x1, Pallas kernels, body(): call(basis_kernel, 'basis', [VMEM] * 3, [((32, 128), F32)])  5.03 us
    pallas_call x1, Pallas kernels, body(): call(load_kernel, 'load', [SMEM] + [HBM] * 4, [((terms, 2, 8, 32, 512), B...  4.4 us
    pallas_call x1, Pallas kernels, body(): call(far_kernel, 'far', [SMEM] + [VMEM] * 5, [products, ((256, 640), BF)]...  2.88 us
    ppermute x1, starting transfers between devices, body(): lax.ppermute(gram, 'op', swap)  2.23 us
    pallas_call x1, Pallas kernels, body(): call(near_kernel, 'near', [SMEM] + [VMEM] * 3, [products], limit=4, flops...  1.92 us
    ppermute x1, starting transfers between devices, body(): far = lax.ppermute(near, 'op', swap)  1.88 us
  transfers between devices with their start and end apart: 4, of which 2 were waited for; matrix products, arithmetic and copies ran while one was open for 0% of the time, Pallas kernels for 16%

profile of v3, /device:TPU:5, one launch (start us, length us, event | category | flops | bytes accessed | tf_op | source)
XLA Modules:
  0.0 47.8 jit_solution(213467386166383113)
XLA Ops:
  0.6 5.6 %collective-permute-start = (bf16[512,512]{1,0:T(8,128)(2,1)}, bf16[512,512]{1,0:T(8,128)(2,1)S(1)}, u32[]{:S(2)}, u32[]{:S(2)}) collective-permute-start(bf16[512,512]{1,0:T(8,128)(2,1)} %bitcast.6), channel_id=1, source_target_pairs={{0,1},{17,16},{32,33},{49,48},{64,65},{81,80},{96,97},{113,112},{1... | collective-permute-start | bytes 1572872 | tf_op jit(solution)/shard_map/ppermute | solution.py:192
  6.3 0.0 copy-start
  6.3 0.7 %copy-done = s32[8]{0:T(128)S(1)} copy-done((s32[8]{0:T(128)S(1)}, s32[8]{0:T(128)}, u32[]{:S(2)}) %copy-start) | copy-done | bytes 56
  6.9 4.4 %load.1 = (bf16[8,2,8,32,512]{4,3,2,1,0:T(8,128)(2,1)S(1)}, bf16[4096,512]{1,0:T(8,128)(2,1)S(1)}, bf16[512,128]{1,0:T(8,128)(2,1)S(1)}, bf16[512,4096]{1,0:T(8,128)(2,1)S(1)}) custom-call(s32[8]{0:T(128)S(1)} %copy-done, bf16[8,8,2,32,512]{4,3,2,1,0:T(8,128)(2,1)} %bitcast.4, bf16[4096,512]{1,0:T(8,128)(2,1)} %bitcast.5, bf16[512,512]{1,0:T(8,128)(2,1)} %bitcast.7, ...), custom_call_target="tpu_custom_call" | custom-call | flops 1000 | bytes 18874368 | tf_op jit(solution)/shard_map/load/pallas_call | solution.py:195
  11.3 1.4 %collective-permute-done.near = bf16[512,512]{1,0:T(8,128)(2,1)S(1)} collective-permute-done((bf16[512,512]{1,0:T(8,128)(2,1)}, bf16[512,512]{1,0:T(8,128)(2,1)S(1)}, u32[]{:S(2)}, u32[]{:S(2)}) %collective-permute-start) | collective-permute-done | bytes 524320 | tf_op jit(solution)/shard_map/ppermute | solution.py:192
  12.7 0.0 copy-start.1
  12.7 1.9 %collective-permute-start.1 = (bf16[512,512]{1,0:T(8,128)(2,1)S(1)}, bf16[512,512]{1,0:T(8,128)(2,1)S(1)}, u32[]{:S(2)}, u32[]{:S(2)}) collective-permute-start(bf16[512,512]{1,0:T(8,128)(2,1)S(1)} %collective-permute-done.near), channel_id=1, source_target_pairs={{0,16},{16,0},{32,48},{48,32},{64,80},{80,64},{96,112},{112,96},{1... | collective-permute-start | bytes 1572872 | tf_op jit(solution)/shard_map/ppermute | solution.py:211
  14.6 1.9 %near.1.before = bf16[512,4096]{1,0:T(8,128)(2,1)S(1)} custom-call(s32[8]{0:T(128)S(1)} %copy-done, bf16[512,512]{1,0:T(8,128)(2,1)S(1)} %collective-permute-done.near, bf16[8,2,8,32,512]{4,3,2,1,0:T(8,128)(2,1)S(1)} %get-tuple-element.21.left, bf16[512,4096]{1,0:T(8,128)(2,1)S(1)} %get-tuple-element.24.before), custom_call_target="tpu_custom_call", output_to_operand_aliasing={{}: (3, {})} | custom-call | flops 715827904 | bytes 1000 | tf_op jit(solution)/shard_map/near/pallas_call | solution.py:213
  16.5 0.0 collective-permute-done.1.far
  16.5 0.0 copy-done.1
  16.5 2.9 %far.1 = (bf16[512,4096]{1,0:T(8,128)(2,1)S(1)}, bf16[256,640]{1,0:T(8,128)(2,1)S(1)}) custom-call(s32[8]{0:T(128)S(1)} %copy-done.1, bf16[512,512]{1,0:T(8,128)(2,1)S(1)} %collective-permute-done.1.far, bf16[8,2,8,32,512]{4,3,2,1,0:T(8,128)(2,1)S(1)} %get-tuple-element.21.left, ...), custom_call_target="tpu_custom_call", output_to_operand_aliasing={{0}: (5, {})} | custom-call | flops 2147483648 | bytes 1000 | tf_op jit(solution)/shard_map/far/pallas_call | solution.py:216
  19.4 0.9 %collective-permute-start.2 = (bf16[256,640]{1,0:T(8,128)(2,1)S(1)}, bf16[256,640]{1,0:T(8,128)(2,1)S(1)}, u32[]{:S(2)}, u32[]{:S(2)}) collective-permute-start(bf16[256,640]{1,0:T(8,128)(2,1)S(1)} %get-tuple-element.26), channel_id=1, source_target_pairs={{0,16},{16,0},{32,48},{48,32},{64,80},{80,64},{96,112},{112,96},{1... | collective-permute-start | bytes 983048 | tf_op jit(solution)/shard_map/ppermute | solution.py:225
  20.4 1.4 %mine.1 = f32[256,640]{1,0:T(8,128)S(1)} custom-call(bf16[512,4096]{1,0:T(8,128)(2,1)S(1)} %get-tuple-element.25.inner, bf16[4096,512]{1,0:T(8,128)(2,1)S(1)} %get-tuple-element.22.right, bf16[512,128]{1,0:T(8,128)(2,1)S(1)} %get-tuple-element.23.sketch), custom_call_target="tpu_custom_call" | custom-call | flops 1073741824 | bytes 1000 | tf_op jit(solution)/shard_map/mine/pallas_call | solution.py:226
  21.8 0.0 collective-permute-done.2.got
  21.8 0.1 pack.1
  21.9 16.8 %all_to_all.5.got = bf16[8,384,128]{2,1,0:T(8,128)(2,1)S(1)} all-to-all(bf16[8,384,128]{2,1,0:T(8,128)(2,1)S(1)} %pack.1), channel_id=1, replica_groups={{0,32,64,96,128,160,192,224},{16,48,80,112,144,176,208,240},{1,33,65,97..., dimensions={0} | all-to-all | bytes 1572864 | tf_op jit(solution)/shard_map/all_to_all | solution.py:231
  38.7 0.9 %gram.1 = (bf16[32,512]{1,0:T(8,128)(2,1)}, f32[256,128]{1,0:T(8,128)S(1)}, f32[128,128]{1,0:T(8,128)S(1)}) custom-call(bf16[8,384,128]{2,1,0:T(8,128)(2,1)S(1)} %all_to_all.5.got), custom_call_target="tpu_custom_call" | custom-call | flops 1000 | bytes 1000 | tf_op jit(solution)/shard_map/gram/pallas_call | solution.py:232
  39.6 2.2 %collective-permute-start.3 = (f32[128,128]{1,0:T(8,128)S(1)}, f32[128,128]{1,0:T(8,128)S(1)}, u32[]{:S(2)}, u32[]{:S(2)}) collective-permute-start(f32[128,128]{1,0:T(8,128)S(1)} %get-tuple-element.28.gram), channel_id=1, source_target_pairs={{0,16},{16,0},{32,48},{48,32},{64,80},{80,64},{96,112},{112,96},{1... | collective-permute-start | bytes 196616 | tf_op jit(solution)/shard_map/ppermute | solution.py:236
  41.8 0.9 %collective-permute-done.3.got = f32[128,128]{1,0:T(8,128)S(1)} collective-permute-done((f32[128,128]{1,0:T(8,128)S(1)}, f32[128,128]{1,0:T(8,128)S(1)}, u32[]{:S(2)}, u32[]{:S(2)}) %collective-permute-start.3) | collective-permute-done | bytes 65568 | tf_op jit(solution)/shard_map/ppermute | solution.py:236
  42.7 5.0 %basis.1 = f32[32,128]{1,0:T(8,128)} custom-call(f32[128,128]{1,0:T(8,128)S(1)} %get-tuple-element.28.gram, f32[128,128]{1,0:T(8,128)S(1)} %collective-permute-done.3.got, f32[256,128]{1,0:T(8,128)S(1)} %get-tuple-element.29.half), custom_call_target="tpu_custom_call" | custom-call | flops 1000 | bytes 1000 | tf_op jit(solution)/shard_map/basis/pallas_call | solution.py:235
Async XLA Ops:
  0.6 12.1 %collective-permute-start = (bf16[512,512]{1,0:T(8,128)(2,1)}, bf16[512,512]{1,0:T(8,128)(2,1)S(1)}, u32[]{:S(2)}, u32[]{:S(2)}) collective-permute-start(bf16[512,512]{1,0:T(8,128)(2,1)} %bitcast.6), channel_id=1, source_target_pairs={{0,1},{17,16},{32,33},{49,48},{64,65},{81,80},{96,97},{113,112},{1... | collective-permute-start | bytes 1572872 | tf_op jit(solution)/shard_map/ppermute | solution.py:192
  6.3 0.7 %copy-start = (s32[8]{0:T(128)S(1)}, s32[8]{0:T(128)}, u32[]{:S(2)}) copy-start(s32[8]{0:T(128)} %code.5) | copy-start | bytes 100
  12.7 3.8 %copy-start.1 = (s32[8]{0:T(128)S(1)}, s32[8]{0:T(128)}, u32[]{:S(2)}) copy-start(s32[8]{0:T(128)} %code.5) | copy-start | bytes 100
  12.7 3.8 %collective-permute-start.1 = (bf16[512,512]{1,0:T(8,128)(2,1)S(1)}, bf16[512,512]{1,0:T(8,128)(2,1)S(1)}, u32[]{:S(2)}, u32[]{:S(2)}) collective-permute-start(bf16[512,512]{1,0:T(8,128)(2,1)S(1)} %collective-permute-done.near), channel_id=1, source_target_pairs={{0,16},{16,0},{32,48},{48,32},{64,80},{80,64},{96,112},{112,96},{1... | collective-permute-start | bytes 1572872 | tf_op jit(solution)/shard_map/ppermute | solution.py:211
  19.4 2.3 %collective-permute-start.2 = (bf16[256,640]{1,0:T(8,128)(2,1)S(1)}, bf16[256,640]{1,0:T(8,128)(2,1)S(1)}, u32[]{:S(2)}, u32[]{:S(2)}) collective-permute-start(bf16[256,640]{1,0:T(8,128)(2,1)S(1)} %get-tuple-element.26), channel_id=1, source_target_pairs={{0,16},{16,0},{32,48},{48,32},{64,80},{80,64},{96,112},{112,96},{1... | collective-permute-start | bytes 983048 | tf_op jit(solution)/shard_map/ppermute | solution.py:225
  39.6 3.1 %collective-permute-start.3 = (f32[128,128]{1,0:T(8,128)S(1)}, f32[128,128]{1,0:T(8,128)S(1)}, u32[]{:S(2)}, u32[]{:S(2)}) collective-permute-start(f32[128,128]{1,0:T(8,128)S(1)} %get-tuple-element.28.gram), channel_id=1, source_target_pairs={{0,16},{16,0},{32,48},{48,32},{64,80},{80,64},{96,112},{112,96},{1... | collective-permute-start | bytes 196616 | tf_op jit(solution)/shard_map/ppermute | solution.py:236

commit v4 on v3

--- a/solution.py
+++ b/solution.py
@@ -125,47 +125,43 @@
     half[...] = total
 
 
-def inverse_rows(a, w, ahead):
-    n = len(a)
+def inverse_rows(m, ahead):
+    n = len(m)
     row = lax.broadcasted_iota(jnp.int32, (8, 128), 0)
+    lane = lax.broadcasted_iota(jnp.int32, (8, 128), 1)
     out = []
     for b in range(n):
         near = range(b, min(b + 1 + ahead, n))
-        c = {v: [jnp.broadcast_to(a[v][:, 8 * b + k : 8 * b + k + 1], (8, 128)) for k in range(8)] for v in near}
+        c = {v: [jnp.broadcast_to(m[v][:, 8 * b + k : 8 * b + k + 1], (8, 128)) for k in range(8)] for v in near}
+        here = (lane >= 8 * b) & (lane < 8 * b + 8)
+        for v in range(b, n):
+            m[v] = jnp.where(here, jnp.where(lane == row + 8 * b, 1.0, 0.0) if v == b else 0.0, m[v])
         scale = jnp.zeros((8, 128), F32)
         for k in range(8):
             s = lax.rsqrt(jnp.broadcast_to(c[b][k][k : k + 1, :], (8, 128)))
             scale = jnp.where(row == k, s, scale)
             f = {v: c[v][k] * (s * s) for v in near}
             f[b] = jnp.where(row > k, f[b], 0.0)
-            for m in range(k + 1, 8):
-                q = jnp.broadcast_to(c[b][m][k : k + 1, :], (8, 128))
+            for j in range(k + 1, 8):
+                q = jnp.broadcast_to(c[b][j][k : k + 1, :], (8, 128))
                 for v in near:
-                    c[v][m] = c[v][m] - f[v] * q
-            pa = jnp.broadcast_to(a[b][k : k + 1, :], (8, 128))
-            pw = jnp.broadcast_to(w[b][k : k + 1, :], (8, 128))
+                    c[v][j] = c[v][j] - f[v] * q
+            pivot = jnp.broadcast_to(m[b][k : k + 1, :], (8, 128))
             for v in near:
-                a[v] = a[v] - f[v] * pa
-                w[v] = w[v] - f[v] * pw
-        u, z = a[b] * scale, w[b] * scale
-        out.append(z)
+                m[v] = m[v] - f[v] * pivot
+        u = m[b] * scale
+        out.append(jnp.where(lane < 8 * b + 8, u, 0.0))
         if b + 1 + ahead < n:
-            step = lax.dot_general(
-                u, jnp.concatenate([u, z], 1), (((0,), (0,)), ((), ())), precision=EXACT, preferred_element_type=F32
-            )
+            step = lax.dot_general(u, u, (((0,), (0,)), ((), ())), precision=EXACT, preferred_element_type=F32)
             for v in range(b + 1 + ahead, n):
-                a[v] = a[v] - step[8 * v : 8 * v + 8, :128]
-                w[v] = w[v] - step[8 * v : 8 * v + 8, 128:]
+                m[v] = m[v] - step[8 * v : 8 * v + 8]
     return out
 
 
 def basis_kernel(gram, got, half, basis):
     place = lax.axis_index("op") // 2
-    row = lax.broadcasted_iota(jnp.int32, (8, 128), 0)
-    lane = lax.broadcasted_iota(jnp.int32, (8, 128), 1)
-    a = [gram[8 * v : 8 * v + 8, :] + got[8 * v : 8 * v + 8, :] for v in range(16)]
-    w = [jnp.where(lane == row + 8 * v, 1.0, 0.0).astype(F32) for v in range(16)]
-    inverse = jnp.concatenate(inverse_rows(a, w, 4), 0)
+    m = [gram[8 * v : 8 * v + 8, :] + got[8 * v : 8 * v + 8, :] for v in range(16)]
+    inverse = jnp.concatenate(inverse_rows(m, 3), 0)
     rows = half[pl.ds(pl.multiple_of(place * 32, 32), 32), :]
     basis[...] = math.sqrt(512) * lax.dot_general(
         rows, inverse, (((1,), (1,)), ((), ())), precision=EXACT, preferred_element_type=F32
@@ -176,12 +172,14 @@
     pairs = []
     for s in range(n_sec - 1):
         flip = 8 if s == n_sec // 2 - 1 else 0
-        for o in range(n_op):
-            source, target = (s, s + 1) if o % 2 == 0 else (s + 1, s)
-            pairs.append(((o ^ flip) * n_sec + source, o * n_sec + target))
+        for o in range(0, n_op, 2):
+            up = o if s == 0 else o + 1
+            down = o + 1 if s == n_sec - 2 else o
+            pairs.append(((up ^ flip) * n_sec + s, o * n_sec + s + 1))
+            pairs.append((down * n_sec + s + 1, ((o + 1) ^ flip) * n_sec + s))
     for o in range(0, n_op, 2):
+        pairs.append(((o + 1) * n_sec, o * n_sec))
         pairs.append((o * n_sec + n_sec - 1, (o + 1) * n_sec + n_sec - 1))
-        pairs.append(((o + 1) * n_sec, o * n_sec))
     return pairs
 
 

time: 47.5 us -> 45.7 us (0.962)
  starting transfers between devices: 10.7 us -> 8.09 us
  blocking collectives: 16.8 us -> 15.4 us
  waiting for transfers between devices: 2.28 us -> 3.6 us
  Pallas kernels: 16.6 us -> 17.4 us
    ppermute x1, starting transfers between devices: 5.63 us -> 2.27 us  [body(): near = lax.ppermute(psi[0], ('op', 'sec'), exchanged(n_op, n_sec))]
    ppermute x1, starting transfers between devices: 1.88 us -> 3.45 us  [body(): far = lax.ppermute(near, 'op', swap)]
    all_to_all x1, blocking collectives: 16.8 us -> 15.4 us  [body(): lax.all_to_all(packed, 'op', 0, 0, axis_index_groups=groups, tiled=True)]
    ppermute x1, waiting for transfers between devices: 1.38 us -> 2.47 us  [body(): near = lax.ppermute(psi[0], ('op', 'sec'), exchanged(n_op, n_sec))]
    ppermute x1, starting transfers between devices: 0.95 us -> 0.09 us  [body(): got = lax.ppermute(other, 'op', swap)]
    pallas_call x1, Pallas kernels: 1.92 us -> 2.77 us  [body(): call(near_kernel, 'near', [SMEM] + [VMEM] * 3, [products], limit=4, flops...]
  transfers between devices with their start and end apart: 4 -> 4, of which waited for: 2 -> 3; matrix products, arithmetic and copies ran while one was open for 0% -> 0% of each run, Pallas kernels for 16% -> 18%
where the time goes in v4:
time: 45.7 us; the launch traced here: 45.9 us
  Pallas kernels  17.4 us (38%)
  blocking collectives  15.4 us (34%)
  starting transfers between devices  8.09 us (18%)
  waiting for transfers between devices  3.6 us (8%)
  between operations  0.7 us (2%)
  local copies, waits for them, and re-layouts  0.66 us (1%)
    all_to_all x1, blocking collectives, body(): lax.all_to_all(packed, 'op', 0, 0, axis_index_groups=groups, tiled=True)  15.4 us
    pallas_call x1, Pallas kernels, body(): call(basis_kernel, 'basis', [VMEM] * 3, [((32, 128), F32)])  4.72 us
    pallas_call x1, Pallas kernels, body(): call(load_kernel, 'load', [SMEM] + [HBM] * 4, [((terms, 2, 8, 32, 512), B...  4.23 us
    ppermute x1, starting transfers between devices, body(): far = lax.ppermute(near, 'op', swap)  3.45 us
    pallas_call x1, Pallas kernels, body(): call(far_kernel, 'far', [SMEM] + [VMEM] * 5, [products, ((256, 640), BF)]...  3.31 us
    pallas_call x1, Pallas kernels, body(): call(near_kernel, 'near', [SMEM] + [VMEM] * 3, [products], limit=4, flops...  2.77 us
    ppermute x1, waiting for transfers between devices, body(): near = lax.ppermute(psi[0], ('op', 'sec'), exchanged(n_op, n_sec))  2.47 us
    ppermute x1, starting transfers between devices, body(): lax.ppermute(gram, 'op', swap)  2.28 us
  transfers between devices with their start and end apart: 4, of which 3 were waited for; matrix products, arithmetic and copies ran while one was open for 0% of the time, Pallas kernels for 18%

profile of v4, /device:TPU:5, one launch (start us, length us, event | category | flops | bytes accessed | tf_op | source)
XLA Modules:
  0.0 45.9 jit_solution(18111632700816387336)
XLA Ops:
  0.6 2.3 %collective-permute-start = (bf16[512,512]{1,0:T(8,128)(2,1)}, bf16[512,512]{1,0:T(8,128)(2,1)S(1)}, u32[]{:S(2)}, u32[]{:S(2)}) collective-permute-start(bf16[512,512]{1,0:T(8,128)(2,1)} %bitcast.6), channel_id=1, source_target_pairs={{0,1},{1,16},{32,33},{33,48},{64,65},{65,80},{96,97},{97,112},{128... | collective-permute-start | bytes 1572872 | tf_op jit(solution)/shard_map/ppermute | solution.py:190
  2.9 0.0 copy-start
  2.9 0.7 %copy-done = s32[8]{0:T(128)S(1)} copy-done((s32[8]{0:T(128)S(1)}, s32[8]{0:T(128)}, u32[]{:S(2)}) %copy-start) | copy-done | bytes 56
  3.6 4.2 %load.1 = (bf16[8,2,8,32,512]{4,3,2,1,0:T(8,128)(2,1)S(1)}, bf16[4096,512]{1,0:T(8,128)(2,1)S(1)}, bf16[512,128]{1,0:T(8,128)(2,1)S(1)}, bf16[512,4096]{1,0:T(8,128)(2,1)S(1)}) custom-call(s32[8]{0:T(128)S(1)} %copy-done, bf16[8,8,2,32,512]{4,3,2,1,0:T(8,128)(2,1)} %bitcast.4, bf16[4096,512]{1,0:T(8,128)(2,1)} %bitcast.5, bf16[512,512]{1,0:T(8,128)(2,1)} %bitcast.7, ...), custom_call_target="tpu_custom_call" | custom-call | flops 1000 | bytes 18874368 | tf_op jit(solution)/shard_map/load/pallas_call | solution.py:193
  7.8 2.5 %collective-permute-done.near = bf16[512,512]{1,0:T(8,128)(2,1)S(1)} collective-permute-done((bf16[512,512]{1,0:T(8,128)(2,1)}, bf16[512,512]{1,0:T(8,128)(2,1)S(1)}, u32[]{:S(2)}, u32[]{:S(2)}) %collective-permute-start) | collective-permute-done | bytes 524320 | tf_op jit(solution)/shard_map/ppermute | solution.py:190
  10.3 0.0 copy-start.1
  10.3 3.5 %collective-permute-start.1 = (bf16[512,512]{1,0:T(8,128)(2,1)S(1)}, bf16[512,512]{1,0:T(8,128)(2,1)S(1)}, u32[]{:S(2)}, u32[]{:S(2)}) collective-permute-start(bf16[512,512]{1,0:T(8,128)(2,1)S(1)} %collective-permute-done.near), channel_id=1, source_target_pairs={{0,16},{16,0},{32,48},{48,32},{64,80},{80,64},{96,112},{112,96},{1... | collective-permute-start | bytes 1572872 | tf_op jit(solution)/shard_map/ppermute | solution.py:209
  13.7 2.8 %near.1.before = bf16[512,4096]{1,0:T(8,128)(2,1)S(1)} custom-call(s32[8]{0:T(128)S(1)} %copy-done, bf16[512,512]{1,0:T(8,128)(2,1)S(1)} %collective-permute-done.near, bf16[8,2,8,32,512]{4,3,2,1,0:T(8,128)(2,1)S(1)} %get-tuple-element.21.left, bf16[512,4096]{1,0:T(8,128)(2,1)S(1)} %get-tuple-element.24.before), custom_call_target="tpu_custom_call", output_to_operand_aliasing={{}: (3, {})} | custom-call | flops 715827904 | bytes 1000 | tf_op jit(solution)/shard_map/near/pallas_call | solution.py:211
  16.5 0.0 collective-permute-done.1.far
  16.5 0.0 copy-done.1
  16.5 3.3 %far.1 = (bf16[512,4096]{1,0:T(8,128)(2,1)S(1)}, bf16[256,640]{1,0:T(8,128)(2,1)S(1)}) custom-call(s32[8]{0:T(128)S(1)} %copy-done.1, bf16[512,512]{1,0:T(8,128)(2,1)S(1)} %collective-permute-done.1.far, bf16[8,2,8,32,512]{4,3,2,1,0:T(8,128)(2,1)S(1)} %get-tuple-element.21.left, ...), custom_call_target="tpu_custom_call", output_to_operand_aliasing={{0}: (5, {})} | custom-call | flops 2147483648 | bytes 1000 | tf_op jit(solution)/shard_map/far/pallas_call | solution.py:214
  19.9 0.1 collective-permute-start.2
  20.0 1.4 %mine.1 = f32[256,640]{1,0:T(8,128)S(1)} custom-call(bf16[512,4096]{1,0:T(8,128)(2,1)S(1)} %get-tuple-element.25.inner, bf16[4096,512]{1,0:T(8,128)(2,1)S(1)} %get-tuple-element.22.right, bf16[512,128]{1,0:T(8,128)(2,1)S(1)} %get-tuple-element.23.sketch), custom_call_target="tpu_custom_call" | custom-call | flops 1073741824 | bytes 1000 | tf_op jit(solution)/shard_map/mine/pallas_call | solution.py:224
  21.3 0.2 collective-permute-done.2.got
  21.6 0.1 pack.1
  21.7 15.4 %all_to_all.5.got = bf16[8,384,128]{2,1,0:T(8,128)(2,1)S(1)} all-to-all(bf16[8,384,128]{2,1,0:T(8,128)(2,1)S(1)} %pack.1), channel_id=1, replica_groups={{0,32,64,96,128,160,192,224},{16,48,80,112,144,176,208,240},{1,33,65,97..., dimensions={0} | all-to-all | bytes 1572864 | tf_op jit(solution)/shard_map/all_to_all | solution.py:229
  37.1 0.9 %gram.1 = (bf16[32,512]{1,0:T(8,128)(2,1)}, f32[256,128]{1,0:T(8,128)S(1)}, f32[128,128]{1,0:T(8,128)S(1)}) custom-call(bf16[8,384,128]{2,1,0:T(8,128)(2,1)S(1)} %all_to_all.5.got), custom_call_target="tpu_custom_call" | custom-call | flops 1000 | bytes 1000 | tf_op jit(solution)/shard_map/gram/pallas_call | solution.py:230
  38.0 2.3 %collective-permute-start.3 = (f32[128,128]{1,0:T(8,128)S(1)}, f32[128,128]{1,0:T(8,128)S(1)}, u32[]{:S(2)}, u32[]{:S(2)}) collective-permute-start(f32[128,128]{1,0:T(8,128)S(1)} %get-tuple-element.28.gram), channel_id=1, source_target_pairs={{0,16},{16,0},{32,48},{48,32},{64,80},{80,64},{96,112},{112,96},{1... | collective-permute-start | bytes 196616 | tf_op jit(solution)/shard_map/ppermute | solution.py:234
  40.3 0.9 %collective-permute-done.3.got = f32[128,128]{1,0:T(8,128)S(1)} collective-permute-done((f32[128,128]{1,0:T(8,128)S(1)}, f32[128,128]{1,0:T(8,128)S(1)}, u32[]{:S(2)}, u32[]{:S(2)}) %collective-permute-start.3) | collective-permute-done | bytes 65568 | tf_op jit(solution)/shard_map/ppermute | solution.py:234
  41.2 4.7 %basis.1 = f32[32,128]{1,0:T(8,128)} custom-call(f32[128,128]{1,0:T(8,128)S(1)} %get-tuple-element.28.gram, f32[128,128]{1,0:T(8,128)S(1)} %collective-permute-done.3.got, f32[256,128]{1,0:T(8,128)S(1)} %get-tuple-element.29.half), custom_call_target="tpu_custom_call" | custom-call | flops 1000 | bytes 1000 | tf_op jit(solution)/shard_map/basis/pallas_call | solution.py:233
Async XLA Ops:
  0.6 9.6 %collective-permute-start = (bf16[512,512]{1,0:T(8,128)(2,1)}, bf16[512,512]{1,0:T(8,128)(2,1)S(1)}, u32[]{:S(2)}, u32[]{:S(2)}) collective-permute-start(bf16[512,512]{1,0:T(8,128)(2,1)} %bitcast.6), channel_id=1, source_target_pairs={{0,1},{1,16},{32,33},{33,48},{64,65},{65,80},{96,97},{97,112},{128... | collective-permute-start | bytes 1572872 | tf_op jit(solution)/shard_map/ppermute | solution.py:190
  2.9 0.7 %copy-start = (s32[8]{0:T(128)S(1)}, s32[8]{0:T(128)}, u32[]{:S(2)}) copy-start(s32[8]{0:T(128)} %code.5) | copy-start | bytes 100
  10.3 6.2 %copy-start.1 = (s32[8]{0:T(128)S(1)}, s32[8]{0:T(128)}, u32[]{:S(2)}) copy-start(s32[8]{0:T(128)} %code.5) | copy-start | bytes 100
  10.3 6.2 %collective-permute-start.1 = (bf16[512,512]{1,0:T(8,128)(2,1)S(1)}, bf16[512,512]{1,0:T(8,128)(2,1)S(1)}, u32[]{:S(2)}, u32[]{:S(2)}) collective-permute-start(bf16[512,512]{1,0:T(8,128)(2,1)S(1)} %collective-permute-done.near), channel_id=1, source_target_pairs={{0,16},{16,0},{32,48},{48,32},{64,80},{80,64},{96,112},{112,96},{1... | collective-permute-start | bytes 1572872 | tf_op jit(solution)/shard_map/ppermute | solution.py:209
  19.9 1.7 %collective-permute-start.2 = (bf16[256,640]{1,0:T(8,128)(2,1)S(1)}, bf16[256,640]{1,0:T(8,128)(2,1)S(1)}, u32[]{:S(2)}, u32[]{:S(2)}) collective-permute-start(bf16[256,640]{1,0:T(8,128)(2,1)S(1)} %get-tuple-element.26), channel_id=1, source_target_pairs={{0,16},{16,0},{32,48},{48,32},{64,80},{80,64},{96,112},{112,96},{1... | collective-permute-start | bytes 983048 | tf_op jit(solution)/shard_map/ppermute | solution.py:223
  38.0 3.2 %collective-permute-start.3 = (f32[128,128]{1,0:T(8,128)S(1)}, f32[128,128]{1,0:T(8,128)S(1)}, u32[]{:S(2)}, u32[]{:S(2)}) collective-permute-start(f32[128,128]{1,0:T(8,128)S(1)} %get-tuple-element.28.gram), channel_id=1, source_target_pairs={{0,16},{16,0},{32,48},{48,32},{64,80},{80,64},{96,112},{112,96},{1... | collective-permute-start | bytes 196616 | tf_op jit(solution)/shard_map/ppermute | solution.py:234

commit v5 on v4

--- a/solution.py
+++ b/solution.py
@@ -15,6 +15,7 @@
 VMEM = pl.BlockSpec(memory_space=pltpu.VMEM)
 SMEM = pl.BlockSpec(memory_space=pltpu.SMEM)
 MIB = 2**20
+CHIPS = (0, 4, 5, 1, 2, 6, 7, 3)
 
 
 def call(kernel, name, in_specs, outs, scratch=(), limit=8, flops=1000, bytes_accessed=1000, aliases={}):
@@ -99,14 +100,14 @@
 
 
 def pack_kernel(mine, got, out):
-    for p in range(8):
+    for i, p in enumerate(CHIPS):
         rows = pl.ds(32 * p, 32)
         for j in range(4):
             cols = pl.ds(128 * j, 128)
-            out[p, 32 * j : 32 * j + 32, :] = (mine[rows, cols] + got[rows, cols].astype(F32)).astype(BF)
+            out[i, 32 * j : 32 * j + 32, :] = (mine[rows, cols] + got[rows, cols].astype(F32)).astype(BF)
     some = (mine[:, 512:] + got[:, 512:].astype(F32)).astype(BF)
-    for p in range(8):
-        out[p, 128:, :] = some
+    for i in range(8):
+        out[i, 128:, :] = some
 
 
 def sum_kernel(got, sigma, half, gram):
@@ -125,35 +126,38 @@
     half[...] = total
 
 
-def inverse_rows(m, ahead):
-    n = len(m)
+def inverse_rows(m, window, ahead):
+    n, size = len(m), 8 * window
     row = lax.broadcasted_iota(jnp.int32, (8, 128), 0)
     lane = lax.broadcasted_iota(jnp.int32, (8, 128), 1)
     out = []
-    for b in range(n):
-        near = range(b, min(b + 1 + ahead, n))
-        c = {v: [jnp.broadcast_to(m[v][:, 8 * b + k : 8 * b + k + 1], (8, 128)) for k in range(8)] for v in near}
-        here = (lane >= 8 * b) & (lane < 8 * b + 8)
+    for b in range(0, n, window):
+        top, near, base = range(b, b + window), range(b, min(b + window + ahead, n)), 8 * b
+        c = {v: [jnp.broadcast_to(m[v][:, base + k : base + k + 1], (8, 128)) for k in range(size)] for v in near}
+        here = (lane >= base) & (lane < base + size)
         for v in range(b, n):
-            m[v] = jnp.where(here, jnp.where(lane == row + 8 * b, 1.0, 0.0) if v == b else 0.0, m[v])
-        scale = jnp.zeros((8, 128), F32)
-        for k in range(8):
-            s = lax.rsqrt(jnp.broadcast_to(c[b][k][k : k + 1, :], (8, 128)))
-            scale = jnp.where(row == k, s, scale)
-            f = {v: c[v][k] * (s * s) for v in near}
-            f[b] = jnp.where(row > k, f[b], 0.0)
-            for j in range(k + 1, 8):
-                q = jnp.broadcast_to(c[b][j][k : k + 1, :], (8, 128))
-                for v in near:
+            m[v] = jnp.where(here, jnp.where(lane == row + 8 * v, 1.0, 0.0) if v in top else 0.0, m[v])
+        scale = {v: jnp.zeros((8, 128), F32) for v in top}
+        for k in range(size):
+            h, i = b + k // 8, k % 8
+            s = lax.rsqrt(jnp.broadcast_to(c[h][k][i : i + 1, :], (8, 128)))
+            scale[h] = jnp.where(row == i, s, scale[h])
+            below = [v for v in near if v >= h]
+            f = {v: c[v][k] * (s * s) for v in below}
+            f[h] = jnp.where(row > i, f[h], 0.0)
+            for j in range(k + 1, size):
+                q = jnp.broadcast_to(c[h][j][i : i + 1, :], (8, 128))
+                for v in below:
                     c[v][j] = c[v][j] - f[v] * q
-            pivot = jnp.broadcast_to(m[b][k : k + 1, :], (8, 128))
-            for v in near:
+            pivot = jnp.broadcast_to(m[h][i : i + 1, :], (8, 128))
+            for v in below:
                 m[v] = m[v] - f[v] * pivot
-        u = m[b] * scale
-        out.append(jnp.where(lane < 8 * b + 8, u, 0.0))
-        if b + 1 + ahead < n:
+        done = [m[v] * scale[v] for v in top]
+        out += [jnp.where(lane < 8 * v + 8, u, 0.0) for v, u in zip(top, done)]
+        if b + window + ahead < n:
+            u = jnp.concatenate(done, 0)
             step = lax.dot_general(u, u, (((0,), (0,)), ((), ())), precision=EXACT, preferred_element_type=F32)
-            for v in range(b + 1 + ahead, n):
+            for v in range(b + window + ahead, n):
                 m[v] = m[v] - step[8 * v : 8 * v + 8]
     return out
 
@@ -161,7 +165,7 @@
 def basis_kernel(gram, got, half, basis):
     place = lax.axis_index("op") // 2
     m = [gram[8 * v : 8 * v + 8, :] + got[8 * v : 8 * v + 8, :] for v in range(16)]
-    inverse = jnp.concatenate(inverse_rows(m, 3), 0)
+    inverse = jnp.concatenate(inverse_rows(m, 2, 2), 0)
     rows = half[pl.ds(pl.multiple_of(place * 32, 32), 32), :]
     basis[...] = math.sqrt(512) * lax.dot_general(
         rows, inverse, (((1,), (1,)), ((), ())), precision=EXACT, preferred_element_type=F32
@@ -225,7 +229,7 @@
         inner, right, sketch
     )
     (packed,) = call(pack_kernel, "pack", [VMEM] * 2, [((8, 384, 128), BF)])(mine, got)
-    groups = [[2 * p + c for p in range(8)] for c in range(2)]
+    groups = [[2 * p + c for p in CHIPS] for c in range(2)]
     parts = lax.all_to_all(packed, "op", 0, 0, axis_index_groups=groups, tiled=True)
     sigma, half, gram = call(
         sum_kernel, "gram", [VMEM], [((32, 512), BF), ((256, 128), F32), ((128, 128), F32)]

time: 45.7 us -> 45.3 us (level); the launches traced: 45.9 us -> 44.7 us
  Pallas kernels: 17.4 us -> 16.3 us
    pallas_call x1, Pallas kernels: 4.72 us -> 4.04 us  [body(): call(basis_kernel, 'basis', [VMEM] * 3, [((32, 128), F32)])]
where the time goes in v5:
time: 45.3 us; the launch traced here: 44.7 us
  Pallas kernels  16.3 us (36%)
  blocking collectives  15.3 us (34%)
  starting transfers between devices  8.14 us (18%)
  waiting for transfers between devices  3.6 us (8%)
  between operations  0.7 us (2%)
  local copies, waits for them, and re-layouts  0.66 us (1%)
    all_to_all x1, blocking collectives, body(): lax.all_to_all(packed, 'op', 0, 0, axis_index_groups=groups, tiled=True)  15.3 us
    pallas_call x1, Pallas kernels, body(): call(load_kernel, 'load', [SMEM] + [HBM] * 4, [((terms, 2, 8, 32, 512), B...  4.23 us
    pallas_call x1, Pallas kernels, body(): call(basis_kernel, 'basis', [VMEM] * 3, [((32, 128), F32)])  4.04 us
    ppermute x1, starting transfers between devices, body(): far = lax.ppermute(near, 'op', swap)  3.45 us
    pallas_call x1, Pallas kernels, body(): call(far_kernel, 'far', [SMEM] + [VMEM] * 5, [products, ((256, 640), BF)]...  3.31 us
    ppermute x1, waiting for transfers between devices, body(): near = lax.ppermute(psi[0], ('op', 'sec'), exchanged(n_op, n_sec))  2.47 us
    pallas_call x1, Pallas kernels, body(): call(near_kernel, 'near', [SMEM] + [VMEM] * 3, [products], limit=4, flops...  2.35 us
    ppermute x1, starting transfers between devices, body(): lax.ppermute(gram, 'op', swap)  2.32 us
  transfers between devices with their start and end apart: 4, of which 3 were waited for; matrix products, arithmetic and copies ran while one was open for 0% of the time, Pallas kernels for 18%

profile of v5, /device:TPU:5, one launch (start us, length us, event | category | flops | bytes accessed | tf_op | source)
XLA Modules:
  0.0 44.7 jit_solution(16717132004810742299)
XLA Ops:
  0.6 2.3 %collective-permute-start = (bf16[512,512]{1,0:T(8,128)(2,1)}, bf16[512,512]{1,0:T(8,128)(2,1)S(1)}, u32[]{:S(2)}, u32[]{:S(2)}) collective-permute-start(bf16[512,512]{1,0:T(8,128)(2,1)} %bitcast.6), channel_id=1, source_target_pairs={{0,1},{1,16},{32,33},{33,48},{64,65},{65,80},{96,97},{97,112},{128... | collective-permute-start | bytes 1572872 | tf_op jit(solution)/shard_map/ppermute | solution.py:194
  2.9 0.0 copy-start
  2.9 0.7 %copy-done = s32[8]{0:T(128)S(1)} copy-done((s32[8]{0:T(128)S(1)}, s32[8]{0:T(128)}, u32[]{:S(2)}) %copy-start) | copy-done | bytes 56
  3.6 4.2 %load.1 = (bf16[8,2,8,32,512]{4,3,2,1,0:T(8,128)(2,1)S(1)}, bf16[4096,512]{1,0:T(8,128)(2,1)S(1)}, bf16[512,128]{1,0:T(8,128)(2,1)S(1)}, bf16[512,4096]{1,0:T(8,128)(2,1)S(1)}) custom-call(s32[8]{0:T(128)S(1)} %copy-done, bf16[8,8,2,32,512]{4,3,2,1,0:T(8,128)(2,1)} %bitcast.4, bf16[4096,512]{1,0:T(8,128)(2,1)} %bitcast.5, bf16[512,512]{1,0:T(8,128)(2,1)} %bitcast.7, ...), custom_call_target="tpu_custom_call" | custom-call | flops 1000 | bytes 18874368 | tf_op jit(solution)/shard_map/load/pallas_call | solution.py:197
  7.8 2.5 %collective-permute-done.near = bf16[512,512]{1,0:T(8,128)(2,1)S(1)} collective-permute-done((bf16[512,512]{1,0:T(8,128)(2,1)}, bf16[512,512]{1,0:T(8,128)(2,1)S(1)}, u32[]{:S(2)}, u32[]{:S(2)}) %collective-permute-start) | collective-permute-done | bytes 524320 | tf_op jit(solution)/shard_map/ppermute | solution.py:194
  10.3 0.0 copy-start.1
  10.3 3.5 %collective-permute-start.1 = (bf16[512,512]{1,0:T(8,128)(2,1)S(1)}, bf16[512,512]{1,0:T(8,128)(2,1)S(1)}, u32[]{:S(2)}, u32[]{:S(2)}) collective-permute-start(bf16[512,512]{1,0:T(8,128)(2,1)S(1)} %collective-permute-done.near), channel_id=1, source_target_pairs={{0,16},{16,0},{32,48},{48,32},{64,80},{80,64},{96,112},{112,96},{1... | collective-permute-start | bytes 1572872 | tf_op jit(solution)/shard_map/ppermute | solution.py:213
  13.7 2.3 %near.1.before = bf16[512,4096]{1,0:T(8,128)(2,1)S(1)} custom-call(s32[8]{0:T(128)S(1)} %copy-done, bf16[512,512]{1,0:T(8,128)(2,1)S(1)} %collective-permute-done.near, bf16[8,2,8,32,512]{4,3,2,1,0:T(8,128)(2,1)S(1)} %get-tuple-element.21.left, bf16[512,4096]{1,0:T(8,128)(2,1)S(1)} %get-tuple-element.24.before), custom_call_target="tpu_custom_call", output_to_operand_aliasing={{}: (3, {})} | custom-call | flops 715827904 | bytes 1000 | tf_op jit(solution)/shard_map/near/pallas_call | solution.py:215
  16.1 0.0 collective-permute-done.1.far
  16.1 0.0 copy-done.1
  16.1 3.3 %far.1 = (bf16[512,4096]{1,0:T(8,128)(2,1)S(1)}, bf16[256,640]{1,0:T(8,128)(2,1)S(1)}) custom-call(s32[8]{0:T(128)S(1)} %copy-done.1, bf16[512,512]{1,0:T(8,128)(2,1)S(1)} %collective-permute-done.1.far, bf16[8,2,8,32,512]{4,3,2,1,0:T(8,128)(2,1)S(1)} %get-tuple-element.21.left, ...), custom_call_target="tpu_custom_call", output_to_operand_aliasing={{0}: (5, {})} | custom-call | flops 2147483648 | bytes 1000 | tf_op jit(solution)/shard_map/far/pallas_call | solution.py:218
  19.4 0.1 collective-permute-start.2
  19.5 1.4 %mine.1 = f32[256,640]{1,0:T(8,128)S(1)} custom-call(bf16[512,4096]{1,0:T(8,128)(2,1)S(1)} %get-tuple-element.25.inner, bf16[4096,512]{1,0:T(8,128)(2,1)S(1)} %get-tuple-element.22.right, bf16[512,128]{1,0:T(8,128)(2,1)S(1)} %get-tuple-element.23.sketch), custom_call_target="tpu_custom_call" | custom-call | flops 1073741824 | bytes 1000 | tf_op jit(solution)/shard_map/mine/pallas_call | solution.py:228
  20.9 0.2 collective-permute-done.2.got
  21.1 0.1 pack.1
  21.2 15.3 %all_to_all.5.got = bf16[8,384,128]{2,1,0:T(8,128)(2,1)S(1)} all-to-all(bf16[8,384,128]{2,1,0:T(8,128)(2,1)S(1)} %pack.1), channel_id=1, replica_groups={{0,128,160,32,64,192,224,96},{16,144,176,48,80,208,240,112},{1,129,161,..., dimensions={0} | all-to-all | bytes 1572864 | tf_op jit(solution)/shard_map/all_to_all | solution.py:233
  36.5 0.9 %gram.1 = (bf16[32,512]{1,0:T(8,128)(2,1)}, f32[256,128]{1,0:T(8,128)S(1)}, f32[128,128]{1,0:T(8,128)S(1)}) custom-call(bf16[8,384,128]{2,1,0:T(8,128)(2,1)S(1)} %all_to_all.5.got), custom_call_target="tpu_custom_call" | custom-call | flops 1000 | bytes 1000 | tf_op jit(solution)/shard_map/gram/pallas_call | solution.py:234
  37.5 2.3 %collective-permute-start.3 = (f32[128,128]{1,0:T(8,128)S(1)}, f32[128,128]{1,0:T(8,128)S(1)}, u32[]{:S(2)}, u32[]{:S(2)}) collective-permute-start(f32[128,128]{1,0:T(8,128)S(1)} %get-tuple-element.28.gram), channel_id=1, source_target_pairs={{0,16},{16,0},{32,48},{48,32},{64,80},{80,64},{96,112},{112,96},{1... | collective-permute-start | bytes 196616 | tf_op jit(solution)/shard_map/ppermute | solution.py:238
  39.8 0.9 %collective-permute-done.3.got = f32[128,128]{1,0:T(8,128)S(1)} collective-permute-done((f32[128,128]{1,0:T(8,128)S(1)}, f32[128,128]{1,0:T(8,128)S(1)}, u32[]{:S(2)}, u32[]{:S(2)}) %collective-permute-start.3) | collective-permute-done | bytes 65568 | tf_op jit(solution)/shard_map/ppermute | solution.py:238
  40.7 4.0 %basis.1 = f32[32,128]{1,0:T(8,128)} custom-call(f32[128,128]{1,0:T(8,128)S(1)} %get-tuple-element.28.gram, f32[128,128]{1,0:T(8,128)S(1)} %collective-permute-done.3.got, f32[256,128]{1,0:T(8,128)S(1)} %get-tuple-element.29.half), custom_call_target="tpu_custom_call" | custom-call | flops 1000 | bytes 1000 | tf_op jit(solution)/shard_map/basis/pallas_call | solution.py:237
Async XLA Ops:
  0.6 9.6 %collective-permute-start = (bf16[512,512]{1,0:T(8,128)(2,1)}, bf16[512,512]{1,0:T(8,128)(2,1)S(1)}, u32[]{:S(2)}, u32[]{:S(2)}) collective-permute-start(bf16[512,512]{1,0:T(8,128)(2,1)} %bitcast.6), channel_id=1, source_target_pairs={{0,1},{1,16},{32,33},{33,48},{64,65},{65,80},{96,97},{97,112},{128... | collective-permute-start | bytes 1572872 | tf_op jit(solution)/shard_map/ppermute | solution.py:194
  2.9 0.7 %copy-start = (s32[8]{0:T(128)S(1)}, s32[8]{0:T(128)}, u32[]{:S(2)}) copy-start(s32[8]{0:T(128)} %code.5) | copy-start | bytes 100
  10.3 5.8 %copy-start.1 = (s32[8]{0:T(128)S(1)}, s32[8]{0:T(128)}, u32[]{:S(2)}) copy-start(s32[8]{0:T(128)} %code.5) | copy-start | bytes 100
  10.3 5.8 %collective-permute-start.1 = (bf16[512,512]{1,0:T(8,128)(2,1)S(1)}, bf16[512,512]{1,0:T(8,128)(2,1)S(1)}, u32[]{:S(2)}, u32[]{:S(2)}) collective-permute-start(bf16[512,512]{1,0:T(8,128)(2,1)S(1)} %collective-permute-done.near), channel_id=1, source_target_pairs={{0,16},{16,0},{32,48},{48,32},{64,80},{80,64},{96,112},{112,96},{1... | collective-permute-start | bytes 1572872 | tf_op jit(solution)/shard_map/ppermute | solution.py:213
  19.4 1.7 %collective-permute-start.2 = (bf16[256,640]{1,0:T(8,128)(2,1)S(1)}, bf16[256,640]{1,0:T(8,128)(2,1)S(1)}, u32[]{:S(2)}, u32[]{:S(2)}) collective-permute-start(bf16[256,640]{1,0:T(8,128)(2,1)S(1)} %get-tuple-element.26), channel_id=1, source_target_pairs={{0,16},{16,0},{32,48},{48,32},{64,80},{80,64},{96,112},{112,96},{1... | collective-permute-start | bytes 983048 | tf_op jit(solution)/shard_map/ppermute | solution.py:227
  37.5 3.2 %collective-permute-start.3 = (f32[128,128]{1,0:T(8,128)S(1)}, f32[128,128]{1,0:T(8,128)S(1)}, u32[]{:S(2)}, u32[]{:S(2)}) collective-permute-start(f32[128,128]{1,0:T(8,128)S(1)} %get-tuple-element.28.gram), channel_id=1, source_target_pairs={{0,16},{16,0},{32,48},{48,32},{64,80},{80,64},{96,112},{112,96},{1... | collective-permute-start | bytes 196616 | tf_op jit(solution)/shard_map/ppermute | solution.py:238

commit v6 on v5

--- a/solution.py
+++ b/solution.py
@@ -110,20 +110,23 @@
         out[i, 128:, :] = some
 
 
-def sum_kernel(got, sigma, half, gram):
+def sum_kernel(got, half, gram):
+    total = got[0, 128:, :].astype(F32)
+    for p in range(1, 8):
+        total += got[p, 128:, :].astype(F32)
+    gram[...] = lax.dot_general(
+        total, total, (((0,), (0,)), ((), ())), precision=EXACT, preferred_element_type=F32
+    )
+    half[...] = total
+
+
+def sigma_kernel(got, sigma):
     for j in range(4):
         rows = pl.ds(32 * j, 32)
         total = got[0, rows, :].astype(F32)
         for p in range(1, 8):
             total += got[p, rows, :].astype(F32)
         sigma[:, 128 * j : 128 * j + 128] = total.astype(BF)
-    total = got[0, 128:, :].astype(F32)
-    for p in range(1, 8):
-        total += got[p, 128:, :].astype(F32)
-    gram[...] = lax.dot_general(
-        total, total, (((0,), (0,)), ((), ())), precision=EXACT, preferred_element_type=F32
-    )
-    half[...] = total
 
 
 def inverse_rows(m, window, ahead):
@@ -231,12 +234,10 @@
     (packed,) = call(pack_kernel, "pack", [VMEM] * 2, [((8, 384, 128), BF)])(mine, got)
     groups = [[2 * p + c for p in CHIPS] for c in range(2)]
     parts = lax.all_to_all(packed, "op", 0, 0, axis_index_groups=groups, tiled=True)
-    sigma, half, gram = call(
-        sum_kernel, "gram", [VMEM], [((32, 512), BF), ((256, 128), F32), ((128, 128), F32)]
-    )(parts)
-    (basis,) = call(basis_kernel, "basis", [VMEM] * 3, [((32, 128), F32)])(
-        gram, lax.ppermute(gram, "op", swap), half
-    )
+    half, gram = call(sum_kernel, "gram", [VMEM], [((256, 128), F32), ((128, 128), F32)])(parts)
+    other_gram = lax.ppermute(gram, "op", swap)
+    (sigma,) = call(sigma_kernel, "sigma", [VMEM], [((32, 512), BF)], bytes_accessed=4 * MIB)(parts)
+    (basis,) = call(basis_kernel, "basis", [VMEM] * 3, [((32, 128), F32)])(gram, other_gram, half)
     return sigma, basis
 
 

time: 45.3 us -> 45.6 us (level)
  blocking collectives: 15.3 us -> 16.6 us
  waiting for transfers between devices: 3.6 us -> 2.98 us
    all_to_all x1, blocking collectives: 15.3 us -> 16.6 us  [body(): lax.all_to_all(packed, 'op', 0, 0, axis_index_groups=groups, tiled=True)]
    pallas_call x1, Pallas kernels: 2.35 us -> 1.49 us  [body(): call(near_kernel, 'near', [SMEM] + [VMEM] * 3, [products], limit=4, flops...]
    ppermute x1, waiting for transfers between devices: 0.9 us -> 0.25 us  [body(): other_gram = lax.ppermute(gram, 'op', swap)]
    pallas_call x1 -> x2, Pallas kernels: 0.93 us -> 1 us  [the longest x1 0.65 us: body(): call(sigma_kernel, 'sigma', [VMEM], [((32, 512), BF)], bytes_accessed=4 *...]
  transfers between devices with their start and end apart: 4 -> 4, of which waited for: 3 -> 3; matrix products, arithmetic and copies ran while one was open for 0% -> 0% of each run, Pallas kernels for 18% -> 17%
where the time goes in v6:
time: 45.6 us; the launch traced here: 45.3 us
  blocking collectives  16.6 us (36%)
  Pallas kernels  16 us (35%)
  starting transfers between devices  8.4 us (18%)
  waiting for transfers between devices  2.98 us (7%)
  between operations  0.69 us (2%)
  local copies, waits for them, and re-layouts  0.66 us (1%)
    all_to_all x1, blocking collectives, body(): lax.all_to_all(packed, 'op', 0, 0, axis_index_groups=groups, tiled=True)  16.6 us
    pallas_call x1, Pallas kernels, body(): call(load_kernel, 'load', [SMEM] + [HBM] * 4, [((terms, 2, 8, 32, 512), B...  4.23 us
    pallas_call x1, Pallas kernels, body(): call(basis_kernel, 'basis', [VMEM] * 3, [((32, 128), F32)])  4.04 us
    pallas_call x1, Pallas kernels, body(): call(far_kernel, 'far', [SMEM] + [VMEM] * 5, [products, ((256, 640), BF)]...  3.74 us
    ppermute x1, starting transfers between devices, body(): far = lax.ppermute(near, 'op', swap)  3.45 us
    ppermute x1, starting transfers between devices, body(): other_gram = lax.ppermute(gram, 'op', swap)  2.59 us
    ppermute x1, waiting for transfers between devices, body(): near = lax.ppermute(psi[0], ('op', 'sec'), exchanged(n_op, n_sec))  2.47 us
    ppermute x1, starting transfers between devices, body(): near = lax.ppermute(psi[0], ('op', 'sec'), exchanged(n_op, n_sec))  2.27 us
  transfers between devices with their start and end apart: 4, of which 3 were waited for; matrix products, arithmetic and copies ran while one was open for 0% of the time, Pallas kernels for 17%

profile of v6, /device:TPU:5, one launch (start us, length us, event | category | flops | bytes accessed | tf_op | source)
XLA Modules:
  0.0 45.3 jit_solution(5227848257974454155)
XLA Ops:
  0.6 2.3 %collective-permute-start = (bf16[512,512]{1,0:T(8,128)(2,1)}, bf16[512,512]{1,0:T(8,128)(2,1)S(1)}, u32[]{:S(2)}, u32[]{:S(2)}) collective-permute-start(bf16[512,512]{1,0:T(8,128)(2,1)} %bitcast.6), channel_id=1, source_target_pairs={{0,1},{1,16},{32,33},{33,48},{64,65},{65,80},{96,97},{97,112},{128... | collective-permute-start | bytes 1572872 | tf_op jit(solution)/shard_map/ppermute | solution.py:197
  2.9 0.0 copy-start
  2.9 0.7 %copy-done = s32[8]{0:T(128)S(1)} copy-done((s32[8]{0:T(128)S(1)}, s32[8]{0:T(128)}, u32[]{:S(2)}) %copy-start) | copy-done | bytes 56
  3.6 4.2 %load.1 = (bf16[8,2,8,32,512]{4,3,2,1,0:T(8,128)(2,1)S(1)}, bf16[4096,512]{1,0:T(8,128)(2,1)S(1)}, bf16[512,128]{1,0:T(8,128)(2,1)S(1)}, bf16[512,4096]{1,0:T(8,128)(2,1)S(1)}) custom-call(s32[8]{0:T(128)S(1)} %copy-done, bf16[8,8,2,32,512]{4,3,2,1,0:T(8,128)(2,1)} %bitcast.4, bf16[4096,512]{1,0:T(8,128)(2,1)} %bitcast.5, bf16[512,512]{1,0:T(8,128)(2,1)} %bitcast.7, ...), custom_call_target="tpu_custom_call" | custom-call | flops 1000 | bytes 18874368 | tf_op jit(solution)/shard_map/load/pallas_call | solution.py:200
  7.8 2.5 %collective-permute-done.near = bf16[512,512]{1,0:T(8,128)(2,1)S(1)} collective-permute-done((bf16[512,512]{1,0:T(8,128)(2,1)}, bf16[512,512]{1,0:T(8,128)(2,1)S(1)}, u32[]{:S(2)}, u32[]{:S(2)}) %collective-permute-start) | collective-permute-done | bytes 524320 | tf_op jit(solution)/shard_map/ppermute | solution.py:197
  10.3 0.0 copy-start.1
  10.3 3.5 %collective-permute-start.1 = (bf16[512,512]{1,0:T(8,128)(2,1)S(1)}, bf16[512,512]{1,0:T(8,128)(2,1)S(1)}, u32[]{:S(2)}, u32[]{:S(2)}) collective-permute-start(bf16[512,512]{1,0:T(8,128)(2,1)S(1)} %collective-permute-done.near), channel_id=1, source_target_pairs={{0,16},{16,0},{32,48},{48,32},{64,80},{80,64},{96,112},{112,96},{1... | collective-permute-start | bytes 1572872 | tf_op jit(solution)/shard_map/ppermute | solution.py:216
  13.7 1.5 %near.1.before = bf16[512,4096]{1,0:T(8,128)(2,1)S(1)} custom-call(s32[8]{0:T(128)S(1)} %copy-done, bf16[512,512]{1,0:T(8,128)(2,1)S(1)} %collective-permute-done.near, bf16[8,2,8,32,512]{4,3,2,1,0:T(8,128)(2,1)S(1)} %get-tuple-element.20.left, bf16[512,4096]{1,0:T(8,128)(2,1)S(1)} %get-tuple-element.23.before), custom_call_target="tpu_custom_call", output_to_operand_aliasing={{}: (3, {})} | custom-call | flops 715827904 | bytes 1000 | tf_op jit(solution)/shard_map/near/pallas_call | solution.py:218
  15.2 0.0 collective-permute-done.1.far
  15.3 0.0 copy-done.1
  15.3 3.7 %far.1 = (bf16[512,4096]{1,0:T(8,128)(2,1)S(1)}, bf16[256,640]{1,0:T(8,128)(2,1)S(1)}) custom-call(s32[8]{0:T(128)S(1)} %copy-done.1, bf16[512,512]{1,0:T(8,128)(2,1)S(1)} %collective-permute-done.1.far, bf16[8,2,8,32,512]{4,3,2,1,0:T(8,128)(2,1)S(1)} %get-tuple-element.20.left, ...), custom_call_target="tpu_custom_call", output_to_operand_aliasing={{0}: (5, {})} | custom-call | flops 2147483648 | bytes 1000 | tf_op jit(solution)/shard_map/far/pallas_call | solution.py:221
  19.0 0.1 collective-permute-start.2
  19.1 1.4 %mine.1 = f32[256,640]{1,0:T(8,128)S(1)} custom-call(bf16[512,4096]{1,0:T(8,128)(2,1)S(1)} %get-tuple-element.24.inner, bf16[4096,512]{1,0:T(8,128)(2,1)S(1)} %get-tuple-element.21.right, bf16[512,128]{1,0:T(8,128)(2,1)S(1)} %get-tuple-element.22.sketch), custom_call_target="tpu_custom_call" | custom-call | flops 1073741824 | bytes 1000 | tf_op jit(solution)/shard_map/mine/pallas_call | solution.py:231
  20.5 0.2 collective-permute-done.2.got
  20.7 0.1 pack.1
  20.8 16.6 %all_to_all.5.got = bf16[8,384,128]{2,1,0:T(8,128)(2,1)S(1)} all-to-all(bf16[8,384,128]{2,1,0:T(8,128)(2,1)S(1)} %pack.1), channel_id=1, replica_groups={{0,128,160,32,64,192,224,96},{16,144,176,48,80,208,240,112},{1,129,161,..., dimensions={0} | all-to-all | bytes 1572864 | tf_op jit(solution)/shard_map/all_to_all | solution.py:236
  37.4 0.3 gram.1
  37.8 2.6 %collective-permute-start.3 = (f32[128,128]{1,0:T(8,128)S(1)}, f32[128,128]{1,0:T(8,128)S(1)}, u32[]{:S(2)}, u32[]{:S(2)}) collective-permute-start(f32[128,128]{1,0:T(8,128)S(1)} %get-tuple-element.26.gram), channel_id=1, source_target_pairs={{0,16},{16,0},{32,48},{48,32},{64,80},{80,64},{96,112},{112,96},{1... | collective-permute-start | bytes 196616 | tf_op jit(solution)/shard_map/ppermute | solution.py:238
  40.3 0.7 %sigma.1 = bf16[32,512]{1,0:T(8,128)(2,1)} custom-call(bf16[8,384,128]{2,1,0:T(8,128)(2,1)S(1)} %all_to_all.5.got), custom_call_target="tpu_custom_call" | custom-call | flops 1000 | bytes 4194304 | tf_op jit(solution)/shard_map/sigma/pallas_call | solution.py:239
  41.0 0.2 collective-permute-done.3.got
  41.2 4.0 %basis.1 = f32[32,128]{1,0:T(8,128)} custom-call(f32[128,128]{1,0:T(8,128)S(1)} %get-tuple-element.26.gram, f32[128,128]{1,0:T(8,128)S(1)} %collective-permute-done.3.got, f32[256,128]{1,0:T(8,128)S(1)} %get-tuple-element.27.half), custom_call_target="tpu_custom_call" | custom-call | flops 1000 | bytes 1000 | tf_op jit(solution)/shard_map/basis/pallas_call | solution.py:240
Async XLA Ops:
  0.6 9.6 %collective-permute-start = (bf16[512,512]{1,0:T(8,128)(2,1)}, bf16[512,512]{1,0:T(8,128)(2,1)S(1)}, u32[]{:S(2)}, u32[]{:S(2)}) collective-permute-start(bf16[512,512]{1,0:T(8,128)(2,1)} %bitcast.6), channel_id=1, source_target_pairs={{0,1},{1,16},{32,33},{33,48},{64,65},{65,80},{96,97},{97,112},{128... | collective-permute-start | bytes 1572872 | tf_op jit(solution)/shard_map/ppermute | solution.py:197
  2.9 0.7 %copy-start = (s32[8]{0:T(128)S(1)}, s32[8]{0:T(128)}, u32[]{:S(2)}) copy-start(s32[8]{0:T(128)} %code.5) | copy-start | bytes 100
  10.3 5.0 %copy-start.1 = (s32[8]{0:T(128)S(1)}, s32[8]{0:T(128)}, u32[]{:S(2)}) copy-start(s32[8]{0:T(128)} %code.5) | copy-start | bytes 100
  10.3 5.0 %collective-permute-start.1 = (bf16[512,512]{1,0:T(8,128)(2,1)S(1)}, bf16[512,512]{1,0:T(8,128)(2,1)S(1)}, u32[]{:S(2)}, u32[]{:S(2)}) collective-permute-start(bf16[512,512]{1,0:T(8,128)(2,1)S(1)} %collective-permute-done.near), channel_id=1, source_target_pairs={{0,16},{16,0},{32,48},{48,32},{64,80},{80,64},{96,112},{112,96},{1... | collective-permute-start | bytes 1572872 | tf_op jit(solution)/shard_map/ppermute | solution.py:216
  19.0 1.7 %collective-permute-start.2 = (bf16[256,640]{1,0:T(8,128)(2,1)S(1)}, bf16[256,640]{1,0:T(8,128)(2,1)S(1)}, u32[]{:S(2)}, u32[]{:S(2)}) collective-permute-start(bf16[256,640]{1,0:T(8,128)(2,1)S(1)} %get-tuple-element.25), channel_id=1, source_target_pairs={{0,16},{16,0},{32,48},{48,32},{64,80},{80,64},{96,112},{112,96},{1... | collective-permute-start | bytes 983048 | tf_op jit(solution)/shard_map/ppermute | solution.py:230
  37.8 3.5 %collective-permute-start.3 = (f32[128,128]{1,0:T(8,128)S(1)}, f32[128,128]{1,0:T(8,128)S(1)}, u32[]{:S(2)}, u32[]{:S(2)}) collective-permute-start(f32[128,128]{1,0:T(8,128)S(1)} %get-tuple-element.26.gram), channel_id=1, source_target_pairs={{0,16},{16,0},{32,48},{48,32},{64,80},{80,64},{96,112},{112,96},{1... | collective-permute-start | bytes 196616 | tf_op jit(solution)/shard_map/ppermute | solution.py:238

commit v7 on v6

--- a/solution.py
+++ b/solution.py
@@ -168,7 +168,7 @@
 def basis_kernel(gram, got, half, basis):
     place = lax.axis_index("op") // 2
     m = [gram[8 * v : 8 * v + 8, :] + got[8 * v : 8 * v + 8, :] for v in range(16)]
-    inverse = jnp.concatenate(inverse_rows(m, 2, 2), 0)
+    inverse = jnp.concatenate(inverse_rows(m, 2, 3), 0)
     rows = half[pl.ds(pl.multiple_of(place * 32, 32), 32), :]
     basis[...] = math.sqrt(512) * lax.dot_general(
         rows, inverse, (((1,), (1,)), ((), ())), precision=EXACT, preferred_element_type=F32

time: 45.6 us -> 45.2 us (level)
  blocking collectives: 16.6 us -> 15.7 us
    all_to_all x1, blocking collectives: 16.6 us -> 15.7 us  [body(): lax.all_to_all(packed, 'op', 0, 0, axis_index_groups=groups, tiled=True)]
    pallas_call x1, Pallas kernels: 1.49 us -> 2.35 us  [body(): call(near_kernel, 'near', [SMEM] + [VMEM] * 3, [products], limit=4, flops...]
  transfers between devices with their start and end apart: 4 -> 4, of which waited for: 3 -> 3; matrix products, arithmetic and copies ran while one was open for 0% -> 0% of each run, Pallas kernels for 17% -> 19%
where the time goes in v7:
time: 45.2 us; the launch traced here: 44.8 us
  Pallas kernels  16.3 us (36%)
  blocking collectives  15.7 us (35%)
  starting transfers between devices  8.4 us (19%)
  waiting for transfers between devices  2.95 us (7%)
  between operations  0.7 us (2%)
  local copies, waits for them, and re-layouts  0.66 us (1%)
    all_to_all x1, blocking collectives, body(): lax.all_to_all(packed, 'op', 0, 0, axis_index_groups=groups, tiled=True)  15.7 us
    pallas_call x1, Pallas kernels, body(): call(load_kernel, 'load', [SMEM] + [HBM] * 4, [((terms, 2, 8, 32, 512), B...  4.23 us
    pallas_call x1, Pallas kernels, body(): call(basis_kernel, 'basis', [VMEM] * 3, [((32, 128), F32)])  3.98 us
    ppermute x1, starting transfers between devices, body(): far = lax.ppermute(near, 'op', swap)  3.45 us
    pallas_call x1, Pallas kernels, body(): call(far_kernel, 'far', [SMEM] + [VMEM] * 5, [products, ((256, 640), BF)]...  3.31 us
    ppermute x1, starting transfers between devices, body(): other_gram = lax.ppermute(gram, 'op', swap)  2.59 us
    ppermute x1, waiting for transfers between devices, body(): near = lax.ppermute(psi[0], ('op', 'sec'), exchanged(n_op, n_sec))  2.47 us
    pallas_call x1, Pallas kernels, body(): call(near_kernel, 'near', [SMEM] + [VMEM] * 3, [products], limit=4, flops...  2.35 us
  transfers between devices with their start and end apart: 4, of which 3 were waited for; matrix products, arithmetic and copies ran while one was open for 0% of the time, Pallas kernels for 19%

profile of v7, /device:TPU:5, one launch (start us, length us, event | category | flops | bytes accessed | tf_op | source)
XLA Modules:
  0.0 44.8 jit_solution(12098938795471859251)
XLA Ops:
  0.6 2.3 %collective-permute-start = (bf16[512,512]{1,0:T(8,128)(2,1)}, bf16[512,512]{1,0:T(8,128)(2,1)S(1)}, u32[]{:S(2)}, u32[]{:S(2)}) collective-permute-start(bf16[512,512]{1,0:T(8,128)(2,1)} %bitcast.6), channel_id=1, source_target_pairs={{0,1},{1,16},{32,33},{33,48},{64,65},{65,80},{96,97},{97,112},{128... | collective-permute-start | bytes 1572872 | tf_op jit(solution)/shard_map/ppermute | solution.py:197
  2.9 0.0 copy-start
  2.9 0.7 %copy-done = s32[8]{0:T(128)S(1)} copy-done((s32[8]{0:T(128)S(1)}, s32[8]{0:T(128)}, u32[]{:S(2)}) %copy-start) | copy-done | bytes 56
  3.6 4.2 %load.1 = (bf16[8,2,8,32,512]{4,3,2,1,0:T(8,128)(2,1)S(1)}, bf16[4096,512]{1,0:T(8,128)(2,1)S(1)}, bf16[512,128]{1,0:T(8,128)(2,1)S(1)}, bf16[512,4096]{1,0:T(8,128)(2,1)S(1)}) custom-call(s32[8]{0:T(128)S(1)} %copy-done, bf16[8,8,2,32,512]{4,3,2,1,0:T(8,128)(2,1)} %bitcast.4, bf16[4096,512]{1,0:T(8,128)(2,1)} %bitcast.5, bf16[512,512]{1,0:T(8,128)(2,1)} %bitcast.7, ...), custom_call_target="tpu_custom_call" | custom-call | flops 1000 | bytes 18874368 | tf_op jit(solution)/shard_map/load/pallas_call | solution.py:200
  7.8 2.5 %collective-permute-done.near = bf16[512,512]{1,0:T(8,128)(2,1)S(1)} collective-permute-done((bf16[512,512]{1,0:T(8,128)(2,1)}, bf16[512,512]{1,0:T(8,128)(2,1)S(1)}, u32[]{:S(2)}, u32[]{:S(2)}) %collective-permute-start) | collective-permute-done | bytes 524320 | tf_op jit(solution)/shard_map/ppermute | solution.py:197
  10.3 0.0 copy-start.1
  10.3 3.5 %collective-permute-start.1 = (bf16[512,512]{1,0:T(8,128)(2,1)S(1)}, bf16[512,512]{1,0:T(8,128)(2,1)S(1)}, u32[]{:S(2)}, u32[]{:S(2)}) collective-permute-start(bf16[512,512]{1,0:T(8,128)(2,1)S(1)} %collective-permute-done.near), channel_id=1, source_target_pairs={{0,16},{16,0},{32,48},{48,32},{64,80},{80,64},{96,112},{112,96},{1... | collective-permute-start | bytes 1572872 | tf_op jit(solution)/shard_map/ppermute | solution.py:216
  13.7 2.3 %near.1.before = bf16[512,4096]{1,0:T(8,128)(2,1)S(1)} custom-call(s32[8]{0:T(128)S(1)} %copy-done, bf16[512,512]{1,0:T(8,128)(2,1)S(1)} %collective-permute-done.near, bf16[8,2,8,32,512]{4,3,2,1,0:T(8,128)(2,1)S(1)} %get-tuple-element.20.left, bf16[512,4096]{1,0:T(8,128)(2,1)S(1)} %get-tuple-element.23.before), custom_call_target="tpu_custom_call", output_to_operand_aliasing={{}: (3, {})} | custom-call | flops 715827904 | bytes 1000 | tf_op jit(solution)/shard_map/near/pallas_call | solution.py:218
  16.1 0.0 collective-permute-done.1.far
  16.1 0.0 copy-done.1
  16.1 3.3 %far.1 = (bf16[512,4096]{1,0:T(8,128)(2,1)S(1)}, bf16[256,640]{1,0:T(8,128)(2,1)S(1)}) custom-call(s32[8]{0:T(128)S(1)} %copy-done.1, bf16[512,512]{1,0:T(8,128)(2,1)S(1)} %collective-permute-done.1.far, bf16[8,2,8,32,512]{4,3,2,1,0:T(8,128)(2,1)S(1)} %get-tuple-element.20.left, ...), custom_call_target="tpu_custom_call", output_to_operand_aliasing={{0}: (5, {})} | custom-call | flops 2147483648 | bytes 1000 | tf_op jit(solution)/shard_map/far/pallas_call | solution.py:221
  19.4 0.1 collective-permute-start.2
  19.5 1.4 %mine.1 = f32[256,640]{1,0:T(8,128)S(1)} custom-call(bf16[512,4096]{1,0:T(8,128)(2,1)S(1)} %get-tuple-element.24.inner, bf16[4096,512]{1,0:T(8,128)(2,1)S(1)} %get-tuple-element.21.right, bf16[512,128]{1,0:T(8,128)(2,1)S(1)} %get-tuple-element.22.sketch), custom_call_target="tpu_custom_call" | custom-call | flops 1073741824 | bytes 1000 | tf_op jit(solution)/shard_map/mine/pallas_call | solution.py:231
  20.9 0.2 collective-permute-done.2.got
  21.1 0.1 pack.1
  21.2 15.7 %all_to_all.5.got = bf16[8,384,128]{2,1,0:T(8,128)(2,1)S(1)} all-to-all(bf16[8,384,128]{2,1,0:T(8,128)(2,1)S(1)} %pack.1), channel_id=1, replica_groups={{0,128,160,32,64,192,224,96},{16,144,176,48,80,208,240,112},{1,129,161,..., dimensions={0} | all-to-all | bytes 1572864 | tf_op jit(solution)/shard_map/all_to_all | solution.py:236
  37.0 0.4 gram.1
  37.3 2.6 %collective-permute-start.3 = (f32[128,128]{1,0:T(8,128)S(1)}, f32[128,128]{1,0:T(8,128)S(1)}, u32[]{:S(2)}, u32[]{:S(2)}) collective-permute-start(f32[128,128]{1,0:T(8,128)S(1)} %get-tuple-element.26.gram), channel_id=1, source_target_pairs={{0,16},{16,0},{32,48},{48,32},{64,80},{80,64},{96,112},{112,96},{1... | collective-permute-start | bytes 196616 | tf_op jit(solution)/shard_map/ppermute | solution.py:238
  39.9 0.7 %sigma.1 = bf16[32,512]{1,0:T(8,128)(2,1)} custom-call(bf16[8,384,128]{2,1,0:T(8,128)(2,1)S(1)} %all_to_all.5.got), custom_call_target="tpu_custom_call" | custom-call | flops 1000 | bytes 4194304 | tf_op jit(solution)/shard_map/sigma/pallas_call | solution.py:239
  40.6 0.2 collective-permute-done.3.got
  40.8 4.0 %basis.1 = f32[32,128]{1,0:T(8,128)} custom-call(f32[128,128]{1,0:T(8,128)S(1)} %get-tuple-element.26.gram, f32[128,128]{1,0:T(8,128)S(1)} %collective-permute-done.3.got, f32[256,128]{1,0:T(8,128)S(1)} %get-tuple-element.27.half), custom_call_target="tpu_custom_call" | custom-call | flops 1000 | bytes 1000 | tf_op jit(solution)/shard_map/basis/pallas_call | solution.py:240
Async XLA Ops:
  0.6 9.6 %collective-permute-start = (bf16[512,512]{1,0:T(8,128)(2,1)}, bf16[512,512]{1,0:T(8,128)(2,1)S(1)}, u32[]{:S(2)}, u32[]{:S(2)}) collective-permute-start(bf16[512,512]{1,0:T(8,128)(2,1)} %bitcast.6), channel_id=1, source_target_pairs={{0,1},{1,16},{32,33},{33,48},{64,65},{65,80},{96,97},{97,112},{128... | collective-permute-start | bytes 1572872 | tf_op jit(solution)/shard_map/ppermute | solution.py:197
  2.9 0.7 %copy-start = (s32[8]{0:T(128)S(1)}, s32[8]{0:T(128)}, u32[]{:S(2)}) copy-start(s32[8]{0:T(128)} %code.5) | copy-start | bytes 100
  10.3 5.8 %copy-start.1 = (s32[8]{0:T(128)S(1)}, s32[8]{0:T(128)}, u32[]{:S(2)}) copy-start(s32[8]{0:T(128)} %code.5) | copy-start | bytes 100
  10.3 5.8 %collective-permute-start.1 = (bf16[512,512]{1,0:T(8,128)(2,1)S(1)}, bf16[512,512]{1,0:T(8,128)(2,1)S(1)}, u32[]{:S(2)}, u32[]{:S(2)}) collective-permute-start(bf16[512,512]{1,0:T(8,128)(2,1)S(1)} %collective-permute-done.near), channel_id=1, source_target_pairs={{0,16},{16,0},{32,48},{48,32},{64,80},{80,64},{96,112},{112,96},{1... | collective-permute-start | bytes 1572872 | tf_op jit(solution)/shard_map/ppermute | solution.py:216
  19.4 1.7 %collective-permute-start.2 = (bf16[256,640]{1,0:T(8,128)(2,1)S(1)}, bf16[256,640]{1,0:T(8,128)(2,1)S(1)}, u32[]{:S(2)}, u32[]{:S(2)}) collective-permute-start(bf16[256,640]{1,0:T(8,128)(2,1)S(1)} %get-tuple-element.25), channel_id=1, source_target_pairs={{0,16},{16,0},{32,48},{48,32},{64,80},{80,64},{96,112},{112,96},{1... | collective-permute-start | bytes 983048 | tf_op jit(solution)/shard_map/ppermute | solution.py:230
  37.3 3.5 %collective-permute-start.3 = (f32[128,128]{1,0:T(8,128)S(1)}, f32[128,128]{1,0:T(8,128)S(1)}, u32[]{:S(2)}, u32[]{:S(2)}) collective-permute-start(f32[128,128]{1,0:T(8,128)S(1)} %get-tuple-element.26.gram), channel_id=1, source_target_pairs={{0,16},{16,0},{32,48},{48,32},{64,80},{80,64},{96,112},{112,96},{1... | collective-permute-start | bytes 196616 | tf_op jit(solution)/shard_map/ppermute | solution.py:238
